TPU v7x, 128 devices: a whole 4x4x4 slice. The times are simulated.
128 devices in a mesh: growth: 4 (over z), lat: 32 (over x, y, core).
Axes of the slice: x: 4, y: 4, z: 4, core: 2. Of those that a mesh axis runs over, the one named last changes fastest.
Arguments:
- source: float32 [32, 1024, 1024], P('growth', 'lat'), may hold values from -4 to 4
- spacing: float32 [32], P('growth'), may hold values from 0.5 to 2
Outputs:
- potential: float32 [32, 1024, 1024], P('growth', 'lat')
All inputs are finite; a program needn't handle non-finite values.
Results may differ from a plain program's by a relative error of at most 0.0003.
Values sent between devices are 32-bit elements; how exact they have to be, the bound alone decides.
No kernel may reach another device: no remote copies, remote signals or barrier semaphores. Data moves between devices by JAX's collectives and lax.ppermute only.
A program may use at most 128 MiB of HBM per device.

v0:
```python
import math

import jax
import jax.numpy as jnp
import numpy as np
from jax import lax
from jax.experimental import pallas as pl
from jax.experimental.pallas import tpu as pltpu
from jax.sharding import PartitionSpec as P

ALL = ("growth", "lat")
LANES = 128
SUB = 8


def table_factors(points):
    k = np.arange(points, dtype=np.int64)[:, None]
    j = np.arange(LANES, dtype=np.int64)[None, :]
    angle = ((2 * j + 1) * k % (4 * points)).astype(np.float64) * (math.pi / (2.0 * points))
    scale = np.where(k == 0, math.sqrt(1.0 / points), math.sqrt(2.0 / points))
    tiles = points // LANES
    period = 2 * tiles
    kk = np.arange(period, dtype=np.int64)[:, None]
    t = np.arange(tiles, dtype=np.int64)[None, :]
    turn = (t * kk % period).astype(np.float64) * (math.pi / tiles)
    wide_cos = np.repeat(np.cos(turn), LANES, axis=1)
    wide_sin = np.repeat(np.sin(turn), LANES, axis=1)
    return [
        a.astype(np.float32)
        for a in (scale * np.cos(angle), scale * np.sin(angle), wide_cos, wide_sin)
    ]


def eigenvalues(points):
    sine = np.sin(np.arange(points, dtype=np.float64) * (math.pi / (2.0 * points)))
    return (4.0 * sine * sine).astype(np.float32)


def split(value):
    high = value.astype(jnp.bfloat16)
    low = (value - high.astype(jnp.float32)).astype(jnp.bfloat16)
    return high, low


def product(left, right, dims):
    def one(a, b):
        return lax.dot_general(a, b, (dims, ((), ())), preferred_element_type=jnp.float32)

    return one(left[0], right[0]) + (one(left[0], right[1]) + one(left[1], right[0]))


def forward_y(source, base_cos, base_sin, wide_cos, wide_sin, out, high, low, rows, sem):
    fetch = pltpu.make_async_copy(source, rows, sem)
    fetch.start()
    points = high.shape[0]
    tiles = points // LANES
    period = wide_cos.shape[0]
    wc = wide_cos[...]
    ws = wide_sin[...]

    @pl.loop(0, points // period)
    def _(i):
        at = pl.ds(pl.multiple_of(i * period, period), period)
        bc = jnp.concatenate([base_cos[at, :]] * tiles, axis=1)
        bs = jnp.concatenate([base_sin[at, :]] * tiles, axis=1)
        h, l = split(bc * wc - bs * ws)
        high[at, :] = h
        low[at, :] = l

    fetch.wait()
    data = split(rows[...])
    step = 256
    for i in range(points // step):
        at = pl.ds(i * step, step)
        out[at, :] = product((high[at, :], low[at, :]), data, ((1,), (1,)))


def swap_groups(v, group):
    low_half = group < 2
    even = group % 2 == 0
    t0 = jnp.where(low_half, v[0], pltpu.roll(v[2], 64, 1))
    t2 = jnp.where(low_half, pltpu.roll(v[0], 64, 1), v[2])
    t1 = jnp.where(low_half, v[1], pltpu.roll(v[3], 64, 1))
    t3 = jnp.where(low_half, pltpu.roll(v[1], 64, 1), v[3])
    w0 = jnp.where(even, t0, pltpu.roll(t1, 32, 1))
    w1 = jnp.where(even, pltpu.roll(t0, 96, 1), t1)
    w2 = jnp.where(even, t2, pltpu.roll(t3, 32, 1))
    w3 = jnp.where(even, pltpu.roll(t2, 96, 1), t3)
    return w0, w1, w2, w3


def middle(
    moved, high, low, own, next1, next2, next3, eig_x, eig_y, out, rows, heights, inverse
):
    slab = own.shape[0]
    slabs = 4
    depth = slab * slabs
    lat = moved.shape[0] // slabs
    width = rows.shape[1]
    grow = lax.axis_index("growth")
    rank = grow * lat + lax.axis_index("lat")
    for k, ref in enumerate((own, next1, next2, next3)):
        at = pl.ds(pl.multiple_of(lax.rem(grow + k, slabs) * slab, slab), slab)
        heights[at, :] = ref[...]
    lane = lax.broadcasted_iota(jnp.int32, (SUB, LANES), 1)
    group = lane // 32

    ey = jnp.sum(jnp.where(lane == rank, eig_y[...], 0.0), axis=1, keepdims=True)
    eigen = jnp.broadcast_to(ey, (SUB, width)) + jnp.broadcast_to(eig_x[...], (SUB, width))

    def wide(row):
        return jnp.concatenate([jnp.broadcast_to(row, (SUB, LANES))] * (width // LANES), axis=1)

    h = [heights[z : z + 1, :] for z in range(depth)]
    zero = jnp.zeros_like(h[0])
    padded = [zero] + h + [zero]
    conduct = [2.0 / (padded[i] + padded[i + 1]) for i in range(depth + 1)]
    inv = None
    for z in range(depth):
        pivot = wide(conduct[z] + conduct[z + 1]) + wide(h[z]) * eigen
        if z:
            pivot = pivot - wide(conduct[z] * conduct[z]) * inv
        inv = 1.0 / pivot
        inverse[pl.ds(z * SUB, SUB), :] = inv

    for g in range(slabs):
        for half in range(2):
            for j in range(lat // 4):
                v = [
                    moved[g * lat + 4 * j + i, :, pl.ds(half * LANES, LANES)] for i in range(4)
                ]
                for q, w in enumerate(swap_groups(v, group)):
                    z = g * slab + half * 4 + q
                    rows[pl.ds(z * SUB, SUB), pl.ds(j * LANES, LANES)] = w

    table = (high[...], low[...])
    rows[...] = product(split(rows[...]), table, ((1,), (1,)))

    partial = None
    for z in range(depth):
        at = pl.ds(z * SUB, SUB)
        value = wide(h[z]) * rows[at, :]
        if z:
            value = value + wide(conduct[z]) * partial
        partial = value * inverse[at, :]
        rows[at, :] = partial
    solved = partial
    for z in reversed(range(depth - 1)):
        at = pl.ds(z * SUB, SUB)
        solved = rows[at, :] + wide(conduct[z + 1]) * inverse[at, :] * solved
        rows[at, :] = solved

    rows[...] = product(split(rows[...]), table, ((1,), (0,)))

    for g in range(slabs):
        for half in range(2):
            for j in range(lat // 4):
                w = [
                    rows[
                        pl.ds((g * slab + half * 4 + q) * SUB, SUB), pl.ds(j * LANES, LANES)
                    ]
                    for q in range(4)
                ]
                for i, v in enumerate(swap_groups(w, group)):
                    out[g * lat + 4 * j + i, :, pl.ds(half * LANES, LANES)] = v


def inverse_y(planes, high, low, out, result, sem):
    table = (high[...], low[...])
    flat = planes[...].T
    count = 4
    step = flat.shape[0] // count
    copies = []
    for i in range(count):
        at = pl.ds(i * step, step)
        result[at, :] = product(split(flat[i * step : (i + 1) * step, :]), table, ((1,), (0,)))
        copies.append(pltpu.make_async_copy(result.at[at, :], out.at[at, :], sem.at[i]))
        copies[-1].start()
    for copy in copies:
        copy.wait()


VMEM = pl.BlockSpec(memory_space=pltpu.VMEM)
HBM = pl.BlockSpec(memory_space=pl.ANY)


def shape(*dims, dtype=jnp.float32):
    return jax.ShapeDtypeStruct(dims, dtype)


def solution(mesh):
    slabs = mesh.shape["growth"]
    lat = mesh.shape["lat"]

    def per_device(source, spacing):
        slab, xlocal, width = source.shape
        devices = slabs * lat
        flat = slab * xlocal
        factors = [jnp.asarray(a) for a in table_factors(width)]
        eig = eigenvalues(width)
        eig_x = jnp.asarray(eig[None, :])
        eig_y = jnp.asarray(eig.reshape(devices, SUB).T)
        own = jnp.broadcast_to(spacing[:, None], (slab, LANES))
        others = [
            lax.ppermute(own, "growth", [((j + k) % slabs, j) for j in range(slabs)])
            for k in range(1, slabs)
        ]
        planes, high, low = pl.pallas_call(
            forward_y,
            out_shape=(
                shape(width, flat),
                shape(width, width, dtype=jnp.bfloat16),
                shape(width, width, dtype=jnp.bfloat16),
            ),
            in_specs=[HBM] + [VMEM] * 4,
            out_specs=(VMEM,) * 3,
            scratch_shapes=[pltpu.VMEM((flat, width), jnp.float32), pltpu.SemaphoreType.DMA],
            compiler_params=pltpu.CompilerParams(vmem_limit_bytes=24 << 20),
            name="forward_y",
        )(source.reshape(flat, width), *factors)
        moved = lax.all_to_all(
            planes.reshape(devices, SUB, flat), ALL, 0, 0, tiled=True
        )
        spatial = pl.pallas_call(
            middle,
            out_shape=shape(devices, SUB, flat),
            in_specs=[VMEM] * 9,
            out_specs=VMEM,
            scratch_shapes=[
                pltpu.VMEM((slab * slabs * SUB, width), jnp.float32),
                pltpu.VMEM((slab * slabs, LANES), jnp.float32),
                pltpu.VMEM((slab * slabs * SUB, width), jnp.float32),
            ],
            compiler_params=pltpu.CompilerParams(vmem_limit_bytes=32 << 20),
            name="middle",
        )(moved, high, low, own, *others, eig_x, eig_y)
        returned = lax.all_to_all(spatial, ALL, 0, 0, tiled=True)
        result = pl.pallas_call(
            inverse_y,
            out_shape=shape(flat, width),
            in_specs=[VMEM] * 3,
            out_specs=HBM,
            scratch_shapes=[
                pltpu.VMEM((flat, width), jnp.float32),
                pltpu.SemaphoreType.DMA((4,)),
            ],
            compiler_params=pltpu.CompilerParams(vmem_limit_bytes=24 << 20),
            name="inverse_y",
        )(returned.reshape(width, flat), high, low)
        return result.reshape(slab, xlocal, width)

    return jax.shard_map(
        per_device,
        mesh=mesh,
        in_specs=(P("growth", "lat", None), P("growth")),
        out_specs=P("growth", "lat", None),
        check_vma=False,
    )
```

profile of v0, /device:TPU:1, one launch (start us, length us, event | category | flops | bytes accessed | tf_op | source)
XLA Modules:
  0.0 75.1 jit_solution(2573898791365933199)
XLA Ops:
  0.0 0.0 copy-start.2
  0.0 1.2 %copy-done.2 = f32[8,32,1024]{2,1,0:T(8,128)S(1)} copy-done((f32[8,32,1024]{2,1,0:T(8,128)S(1)}, f32[8,32,1024]{2,1,0:T(8,128)}, u32[]{:S(2)}) %copy-start.2) | copy-done | bytes 1048600
  1.2 0.0 copy-start.4
  1.2 1.0 %copy-done.4 = f32[1024,128]{1,0:T(8,128)S(1)} copy-done((f32[1024,128]{1,0:T(8,128)S(1)}, f32[1024,128]{1,0:T(8,128)}, u32[]{:S(2)}) %copy-start.4) | copy-done | bytes 524312
  2.3 0.0 copy-start.5
  2.3 1.0 %copy-done.5 = f32[1024,128]{1,0:T(8,128)S(1)} copy-done((f32[1024,128]{1,0:T(8,128)S(1)}, f32[1024,128]{1,0:T(8,128)}, u32[]{:S(2)}) %copy-start.5) | copy-done | bytes 524312
  3.3 0.0 copy-start.6
  3.3 0.8 %copy-done.6 = f32[16,1024]{1,0:T(8,128)S(1)} copy-done((f32[16,1024]{1,0:T(8,128)S(1)}, f32[16,1024]{1,0:T(8,128)}, u32[]{:S(2)}) %copy-start.6) | copy-done | bytes 65560
  4.2 0.0 copy-start.7
  4.2 0.8 %copy-done.7 = f32[16,1024]{1,0:T(8,128)S(1)} copy-done((f32[16,1024]{1,0:T(8,128)S(1)}, f32[16,1024]{1,0:T(8,128)}, u32[]{:S(2)}) %copy-start.7) | copy-done | bytes 65560
  5.0 0.0 copy-start.10
  5.0 0.0 copy-start.8
  5.0 3.1 %forward_y.1 = (f32[1024,256]{1,0:T(8,128)S(1)}, bf16[1024,1024]{1,0:T(8,128)(2,1)S(1)}, bf16[1024,1024]{1,0:T(8,128)(2,1)S(1)}) custom-call(f32[256,1024]{1,0:T(8,128)S(1)} %bitcast.5, f32[1024,128]{1,0:T(8,128)S(1)} %copy-done.4, f32[1024,128]{1,0:T(8,128)S(1)} %copy-done.5, f32[16,1024]{1,0:T(8,128)S(1)} %copy-done.6, f32[16,1024]{1,0:T(8,128)S(1)} %copy-done.7), custom_call_target="tpu_custom_call" | custom-call | tf_op jit(solution)/shard_map/forward_y/pallas_call | solution.py:208
  8.1 0.0 copy-start
  8.1 1.3 %copy-done = bf16[1024,1024]{1,0:T(8,128)(2,1)} copy-done((bf16[1024,1024]{1,0:T(8,128)(2,1)}, bf16[1024,1024]{1,0:T(8,128)(2,1)S(1)}, u32[]{:S(2)}) %copy-start) | copy-done | bytes 2097176
  9.4 1.0 %copy-done.3 = f32[1024,256]{1,0:T(8,128)} copy-done((f32[1024,256]{1,0:T(8,128)}, f32[1024,256]{1,0:T(8,128)S(1)}, u32[]{:S(2)}) %copy-start.3) | copy-done | bytes 1048600
  10.4 11.5 %all-to-all-start = ((f32[128,8,256]{2,1,0:T(8,128)}), f32[128,8,256]{2,1,0:T(8,128)S(1)}, u32[]{:S(2)}, u32[]{:S(2)}) async-start(f32[128,8,256]{2,1,0:T(8,128)} %bitcast.6), calls=%async_computation | async-start | bytes 2097152 | tf_op jit(solution)/shard_map/all_to_all | solution.py:221
  21.9 0.0 copy-done.10
  21.9 0.1 broadcast_in_dim.2.own
  22.0 3.2 %collective-permute-start = (f32[8,128]{1,0:T(8,128)S(1)}, f32[8,128]{1,0:T(8,128)S(1)}, u32[]{:S(2)}, u32[]{:S(2)}) collective-permute-start(f32[8,128]{1,0:T(8,128)S(1)} %broadcast_in_dim.2.own), channel_id=1, source_target_pairs={{32,0},{64,32},{96,64},{0,96},{33,1},{65,33},{97,65},{1,97},{34,2}... | collective-permute-start | bytes 12296 | tf_op jit(solution)/shard_map/ppermute | solution.py:205
  25.2 0.1 collective-permute-start.1
  25.3 0.8 %collective-permute-start.2 = (f32[8,128]{1,0:T(8,128)S(1)}, f32[8,128]{1,0:T(8,128)S(1)}, u32[]{:S(2)}, u32[]{:S(2)}) collective-permute-start(f32[8,128]{1,0:T(8,128)S(1)} %broadcast_in_dim.2.own), channel_id=1, source_target_pairs={{96,0},{0,32},{32,64},{64,96},{97,1},{1,33},{33,65},{65,97},{98,2}... | collective-permute-start | bytes 12296 | tf_op jit(solution)/shard_map/ppermute | solution.py:205
  26.1 0.0 collective-permute-done.next1
  26.1 4.3 %collective-permute-done.1.next2 = f32[8,128]{1,0:T(8,128)S(1)} collective-permute-done((f32[8,128]{1,0:T(8,128)S(1)}, f32[8,128]{1,0:T(8,128)S(1)}, u32[]{:S(2)}, u32[]{:S(2)}) %collective-permute-start.1) | collective-permute-done | bytes 4128 | tf_op jit(solution)/shard_map/ppermute | solution.py:205
  30.4 0.1 collective-permute-done.2.next3
  30.4 10.3 %all-to-all-done.moved = f32[128,8,256]{2,1,0:T(8,128)S(1)} async-done(((f32[128,8,256]{2,1,0:T(8,128)}), f32[128,8,256]{2,1,0:T(8,128)S(1)}, u32[]{:S(2)}, u32[]{:S(2)}) %all-to-all-start) | async-done | bytes 1048608 | tf_op jit(solution)/shard_map/all_to_all | solution.py:221
  40.7 0.0 copy-done.8
  40.7 0.0 copy-done.9
  40.7 1.6 %copy-done.1 = bf16[1024,1024]{1,0:T(8,128)(2,1)S(1)} copy-done((bf16[1024,1024]{1,0:T(8,128)(2,1)S(1)}, bf16[1024,1024]{1,0:T(8,128)(2,1)}, u32[]{:S(2)}) %copy-start.1) | copy-done | bytes 2097176
  42.3 4.2 %middle.1 = f32[128,8,256]{2,1,0:T(8,128)S(1)} custom-call(f32[128,8,256]{2,1,0:T(8,128)S(1)} %all-to-all-done.moved, bf16[1024,1024]{1,0:T(8,128)(2,1)S(1)} %get-tuple-element.9.high, bf16[1024,1024]{1,0:T(8,128)(2,1)S(1)} %copy-done.1, f32[8,128]{1,0:T(8,128)S(1)} %broadcast_in_dim.2.own, f32[8,128]{1,0:T(8,128)S(1)} %collective-permute-done.next1, ...), custom_call_target="tpu_custom_call" | custom-call | tf_op jit(solution)/shard_map/middle/pallas_call | solution.py:224
  46.5 23.3 %all_to_all.10 = f32[128,8,256]{2,1,0:T(8,128)S(1)} all-to-all(f32[128,8,256]{2,1,0:T(8,128)S(1)} %middle.1), channel_id=1, replica_groups=mesh['growth'=4,'lat'=32] {'growth','lat'}, dimensions={0} | all-to-all | bytes 2097152 | tf_op jit(solution)/shard_map/all_to_all | solution.py:237
  69.8 5.3 %inverse_y.1 = f32[256,1024]{1,0:T(8,128)} custom-call(f32[1024,256]{1,0:T(8,128)S(1)} %bitcast.4, bf16[1024,1024]{1,0:T(8,128)(2,1)S(1)} %get-tuple-element.9.high, bf16[1024,1024]{1,0:T(8,128)(2,1)S(1)} %copy-done.1), custom_call_target="tpu_custom_call" | custom-call | tf_op jit(solution)/shard_map/inverse_y/pallas_call | solution.py:238
  (3 shorter events, 0.0 us)
Async XLA Ops:
  0.0 1.2 %copy-start.2 = (f32[8,32,1024]{2,1,0:T(8,128)S(1)}, f32[8,32,1024]{2,1,0:T(8,128)}, u32[]{:S(2)}) copy-start(f32[8,32,1024]{2,1,0:T(8,128)} %param.8) | copy-start | bytes 3145732
  1.2 1.0 %copy-start.4 = (f32[1024,128]{1,0:T(8,128)S(1)}, f32[1024,128]{1,0:T(8,128)}, u32[]{:S(2)}) copy-start(f32[1024,128]{1,0:T(8,128)} %constant.12.clone.base_cos) | copy-start | bytes 1572868
  2.3 1.0 %copy-start.5 = (f32[1024,128]{1,0:T(8,128)S(1)}, f32[1024,128]{1,0:T(8,128)}, u32[]{:S(2)}) copy-start(f32[1024,128]{1,0:T(8,128)} %constant.13.clone.base_sin) | copy-start | bytes 1572868
  3.3 0.8 %copy-start.6 = (f32[16,1024]{1,0:T(8,128)S(1)}, f32[16,1024]{1,0:T(8,128)}, u32[]{:S(2)}) copy-start(f32[16,1024]{1,0:T(8,128)} %constant.14.clone.wide_cos) | copy-start | bytes 196612
  4.2 0.8 %copy-start.7 = (f32[16,1024]{1,0:T(8,128)S(1)}, f32[16,1024]{1,0:T(8,128)}, u32[]{:S(2)}) copy-start(f32[16,1024]{1,0:T(8,128)} %constant.15.clone.wide_sin) | copy-start | bytes 196612
  5.0 16.9 %copy-start.10 = (f32[8]{0:T(128)S(1)}, f32[8]{0:T(128)}, u32[]{:S(2)}) copy-start(f32[8]{0:T(128)} %param.9) | copy-start | bytes 100
  5.0 35.7 %copy-start.8 = (f32[1,1024]{1,0:T(1,128)S(1)}, f32[1,1024]{1,0:T(1,128)}, u32[]{:S(2)}) copy-start(f32[1,1024]{1,0:T(1,128)} %constant.16.clone.eig_x) | copy-start | bytes 12292
  5.0 35.7 %copy-start.9 = (f32[8,128]{1,0:T(8,128)S(1)}, f32[8,128]{1,0:T(8,128)}, u32[]{:S(2)}) copy-start(f32[8,128]{1,0:T(8,128)} %constant.17.clone.eig_y) | copy-start | bytes 12292
  8.1 1.3 %copy-start = (bf16[1024,1024]{1,0:T(8,128)(2,1)}, bf16[1024,1024]{1,0:T(8,128)(2,1)S(1)}, u32[]{:S(2)}) copy-start(bf16[1024,1024]{1,0:T(8,128)(2,1)S(1)} %get-tuple-element.10.low) | copy-start | bytes 6291460
  9.4 1.0 %copy-start.3 = (f32[1024,256]{1,0:T(8,128)}, f32[1024,256]{1,0:T(8,128)S(1)}, u32[]{:S(2)}) copy-start(f32[1024,256]{1,0:T(8,128)S(1)} %get-tuple-element.8) | copy-start | bytes 3145732
  10.4 30.3 %all-to-all-start = ((f32[128,8,256]{2,1,0:T(8,128)}), f32[128,8,256]{2,1,0:T(8,128)S(1)}, u32[]{:S(2)}, u32[]{:S(2)}) async-start(f32[128,8,256]{2,1,0:T(8,128)} %bitcast.6), calls=%async_computation | async-start | bytes 2097152 | tf_op jit(solution)/shard_map/all_to_all | solution.py:221
  22.0 4.1 %collective-permute-start = (f32[8,128]{1,0:T(8,128)S(1)}, f32[8,128]{1,0:T(8,128)S(1)}, u32[]{:S(2)}, u32[]{:S(2)}) collective-permute-start(f32[8,128]{1,0:T(8,128)S(1)} %broadcast_in_dim.2.own), channel_id=1, source_target_pairs={{32,0},{64,32},{96,64},{0,96},{33,1},{65,33},{97,65},{1,97},{34,2}... | collective-permute-start | bytes 12296 | tf_op jit(solution)/shard_map/ppermute | solution.py:205
  25.2 5.2 %collective-permute-start.1 = (f32[8,128]{1,0:T(8,128)S(1)}, f32[8,128]{1,0:T(8,128)S(1)}, u32[]{:S(2)}, u32[]{:S(2)}) collective-permute-start(f32[8,128]{1,0:T(8,128)S(1)} %broadcast_in_dim.2.own), channel_id=1, source_target_pairs={{64,0},{96,32},{0,64},{32,96},{65,1},{97,33},{1,65},{33,97},{66,2}... | collective-permute-start | bytes 12296 | tf_op jit(solution)/shard_map/ppermute | solution.py:205
  25.3 5.1 %collective-permute-start.2 = (f32[8,128]{1,0:T(8,128)S(1)}, f32[8,128]{1,0:T(8,128)S(1)}, u32[]{:S(2)}, u32[]{:S(2)}) collective-permute-start(f32[8,128]{1,0:T(8,128)S(1)} %broadcast_in_dim.2.own), channel_id=1, source_target_pairs={{96,0},{0,32},{32,64},{64,96},{97,1},{1,33},{33,65},{65,97},{98,2}... | collective-permute-start | bytes 12296 | tf_op jit(solution)/shard_map/ppermute | solution.py:205
  40.7 1.6 %copy-start.1 = (bf16[1024,1024]{1,0:T(8,128)(2,1)S(1)}, bf16[1024,1024]{1,0:T(8,128)(2,1)}, u32[]{:S(2)}) copy-start(bf16[1024,1024]{1,0:T(8,128)(2,1)} %copy-done) | copy-start | bytes 6291460
where the time goes:
time: 75.5 us; the launch traced here: 75.1 us
  blocking collectives  23.3 us (31%)
  starting transfers between devices  15.6 us (21%)
  waiting for transfers between devices  14.6 us (19%)
  Pallas kernels  12.6 us (17%)
  local copies, waits for them, and re-layouts  8.95 us (12%)
    all_to_all x1, blocking collectives, per_device(): returned = lax.all_to_all(spatial, ALL, 0, 0, tiled=True)  23.3 us
    all_to_all x1, starting transfers between devices, per_device(): lax.all_to_all(planes.reshape(devices, SUB, flat), ALL, 0, 0, tiled=True)  11.5 us
    all_to_all x1, waiting for transfers between devices, per_device(): lax.all_to_all(planes.reshape(devices, SUB, flat), ALL, 0, 0, tiled=True)  10.3 us
    unnamed x22, local copies, waits for them, and re-layouts  8.88 us
    pallas_call x1, Pallas kernels, per_device(): pl.pallas_call(inverse_y, out_shape=shape(flat, width), in_specs=[VMEM] *...  5.3 us
    ppermute x3, waiting for transfers between devices, per_device(): lax.ppermute(own, 'growth', [((j + k) % slabs, j) for j in range(slabs)])  4.32 us
    pallas_call x1, Pallas kernels, per_device(): pl.pallas_call(middle, out_shape=shape(devices, SUB, flat), in_specs=[VME...  4.21 us
    ppermute x3, starting transfers between devices, per_device(): lax.ppermute(own, 'growth', [((j + k) % slabs, j) for j in range(slabs)])  4.13 us
  transfers between devices with their start and end apart: 4, of which 3 were waited for; matrix products, arithmetic and copies ran while one was open for 0% of the time, Pallas kernels for 0%

commit v1 on v0

v1 whole, which is shorter than its diff:
```python
import math

import jax
import jax.numpy as jnp
import numpy as np
from jax import lax
from jax.experimental import pallas as pl
from jax.experimental.pallas import tpu as pltpu
from jax.sharding import PartitionSpec as P

ALL = ("growth", "lat")
LANES = 128
SUB = 8
GROUP = 32
NT = ((1,), (1,))
NN = ((1,), (0,))


def mode_order(points):
    return np.concatenate([np.arange(0, points, 2), np.arange(1, points, 2)])


def half_table(points):
    k = mode_order(points)[:, None].astype(np.int64)
    j = np.arange(points // 2, dtype=np.int64)[None, :]
    angle = ((2 * j + 1) * k % (4 * points)).astype(np.float64) * (math.pi / (2.0 * points))
    scale = np.where(k == 0, math.sqrt(1.0 / points), math.sqrt(2.0 / points))
    table = (scale * np.cos(angle)).astype(np.float32)
    high = table.astype(jnp.bfloat16)
    low = (table - high.astype(np.float32)).astype(jnp.bfloat16)
    return np.concatenate([high, low], axis=0)


def eigenvalues(points):
    sine = np.sin(mode_order(points).astype(np.float64) * (math.pi / (2.0 * points)))
    return (4.0 * sine * sine).astype(np.float32)


def split(value):
    high = value.astype(jnp.bfloat16)
    low = (value - high.astype(jnp.float32)).astype(jnp.bfloat16)
    return high, low


def product(left, right, dims):
    def one(a, b):
        return lax.dot_general(a, b, (dims, ((), ())), preferred_element_type=jnp.float32)

    return one(left[0], right[0]) + (one(left[0], right[1]) + one(left[1], right[0]))


def parity(table, which):
    n = table.shape[0] // 4
    return (
        table[which * n : (which + 1) * n, :],
        table[(2 + which) * n : (3 + which) * n, :],
    )


def reverse_lanes(value, span):
    lane = lax.broadcasted_iota(jnp.int32, value.shape, 1)
    source = lane // span * span + (span - 1) - lane % span
    return jnp.take_along_axis(value, source, axis=1)


def forward_y(source, table_hbm, out_hbm, rows, table, out, sem, table_sem, out_sem):
    points = rows.shape[1]
    half = points // 2
    tiles = half // LANES
    fetch = pltpu.make_async_copy(source, rows, sem)
    fetch.start()
    tables = []
    for which in range(2):
        for part in range(2):
            at = pl.ds((2 * part + which) * half, half)
            tables.append(
                pltpu.make_async_copy(
                    table_hbm.at[at, :], table.at[at, :], table_sem.at[2 * which + part]
                )
            )
            tables[-1].start()
    fetch.wait()
    first = [rows[:, pl.ds(j * LANES, LANES)] for j in range(tiles)]
    second = [
        reverse_lanes(rows[:, pl.ds((2 * tiles - 1 - j) * LANES, LANES)], LANES)
        for j in range(tiles)
    ]
    folded = (
        split(jnp.concatenate([a + b for a, b in zip(first, second)], axis=1)),
        split(jnp.concatenate([a - b for a, b in zip(first, second)], axis=1)),
    )
    copies = []
    for which in range(2):
        tables[2 * which].wait()
        tables[2 * which + 1].wait()
        at = pl.ds(which * half, half)
        out[at, :] = product(parity(table, which), folded[which], NT)
        copies.append(
            pltpu.make_async_copy(out.at[at, :], out_hbm.at[at, :], out_sem.at[which])
        )
        copies[-1].start()
    for copy in copies:
        copy.wait()


def swap_groups(v, group):
    low_half = group < 2
    even = group % 2 == 0
    t0 = jnp.where(low_half, v[0], pltpu.roll(v[2], 64, 1))
    t2 = jnp.where(low_half, pltpu.roll(v[0], 64, 1), v[2])
    t1 = jnp.where(low_half, v[1], pltpu.roll(v[3], 64, 1))
    t3 = jnp.where(low_half, pltpu.roll(v[1], 64, 1), v[3])
    w0 = jnp.where(even, t0, pltpu.roll(t1, 32, 1))
    w1 = jnp.where(even, pltpu.roll(t0, 96, 1), t1)
    w2 = jnp.where(even, t2, pltpu.roll(t3, 32, 1))
    w3 = jnp.where(even, pltpu.roll(t2, 96, 1), t3)
    return w0, w1, w2, w3


def wide(row, width):
    return jnp.concatenate([jnp.broadcast_to(row, (SUB, LANES))] * (width // LANES), axis=1)


def conductances(h):
    zero = jnp.zeros_like(h[0])
    padded = [zero] + h + [zero]
    return [2.0 / (padded[i] + padded[i + 1]) for i in range(len(h) + 1)]


def fill_pivots(own, next1, next2, next3, eig_x, eig_y, heights, inverse):
    slab = own.shape[0]
    slabs = 4
    depth = slab * slabs
    width = inverse.shape[1]
    grow = lax.axis_index("growth")
    rank = grow * lax.axis_size("lat") + lax.axis_index("lat")
    for k, ref in enumerate((own, next1, next2, next3)):
        at = pl.ds(pl.multiple_of(lax.rem(grow + k, slabs) * slab, slab), slab)
        heights[at, :] = ref[...]
    lane = lax.broadcasted_iota(jnp.int32, (SUB, LANES), 1)
    ey = jnp.sum(jnp.where(lane == rank, eig_y[...], 0.0), axis=1, keepdims=True)
    eigen = jnp.broadcast_to(ey, (SUB, width)) + jnp.broadcast_to(eig_x[...], (SUB, width))
    h = [heights[z : z + 1, :] for z in range(depth)]
    conduct = conductances(h)
    inv = None
    for z in range(depth):
        pivot = wide(conduct[z] + conduct[z + 1], width) + wide(h[z], width) * eigen
        if z:
            pivot = pivot - wide(conduct[z] * conduct[z], width) * inv
        inv = 1.0 / pivot
        inverse[pl.ds(z * SUB, SUB), :] = inv


def middle(
    moved, table, own, next1, next2, next3, eig_x, eig_y, out, rows, heights, inverse
):
    slabs = 4
    fill_pivots(own, next1, next2, next3, eig_x, eig_y, heights, inverse)
    depth = heights.shape[0]
    slab = depth // slabs
    lat = moved.shape[0] // slabs
    width = rows.shape[1]
    half = width // 2
    tiles = half // LANES
    group = lax.broadcasted_iota(jnp.int32, (SUB, LANES), 1) // GROUP
    for g in range(slabs):
        for s in range(2):
            lanes = pl.ds(s * LANES, LANES)
            for j in range(tiles):
                first = swap_groups(
                    [moved[g * lat + 4 * j + i, :, lanes] for i in range(4)], group
                )
                second = swap_groups(
                    [moved[g * lat + lat - 1 - 4 * j - i, :, lanes] for i in range(4)], group
                )
                for q in range(4):
                    z = g * slab + s * 4 + q
                    a = first[q]
                    b = reverse_lanes(second[q], GROUP)
                    at = pl.ds(z * SUB, SUB)
                    rows[at, pl.ds(j * LANES, LANES)] = a + b
                    rows[at, pl.ds(half + j * LANES, LANES)] = a - b
    for which in range(2):
        at = pl.ds(which * half, half)
        rows[:, at] = product(split(rows[:, at]), parity(table, which), NT)

    h = [heights[z : z + 1, :] for z in range(depth)]
    conduct = conductances(h)
    partial = None
    for z in range(depth):
        at = pl.ds(z * SUB, SUB)
        value = wide(h[z], width) * rows[at, :]
        if z:
            value = value + wide(conduct[z], width) * partial
        partial = value * inverse[at, :]
        rows[at, :] = partial
    solved = partial
    for z in reversed(range(depth - 1)):
        at = pl.ds(z * SUB, SUB)
        solved = rows[at, :] + wide(conduct[z + 1], width) * inverse[at, :] * solved
        rows[at, :] = solved

    for which in range(2):
        at = pl.ds(which * half, half)
        rows[:, at] = product(split(rows[:, at]), parity(table, which), NN)
    for g in range(slabs):
        for s in range(2):
            lanes = pl.ds(s * LANES, LANES)
            for j in range(tiles):
                first = []
                second = []
                for q in range(4):
                    at = pl.ds((g * slab + s * 4 + q) * SUB, SUB)
                    a = rows[at, pl.ds(j * LANES, LANES)]
                    b = rows[at, pl.ds(half + j * LANES, LANES)]
                    first.append(a + b)
                    second.append(reverse_lanes(a - b, GROUP))
                for i, v in enumerate(swap_groups(first, group)):
                    out[g * lat + 4 * j + i, :, lanes] = v
                for i, v in enumerate(swap_groups(second, group)):
                    out[g * lat + lat - 1 - 4 * j - i, :, lanes] = v


def inverse_y(planes, table, out, result, sem):
    half = table.shape[1]
    tiles = half // LANES
    flat = planes.shape[1]
    count = flat // LANES
    copies = []
    for i in range(count):
        at = pl.ds(i * LANES, LANES)
        even, odd = (
            product(
                split(planes[pl.ds(which * half, half), at].T), parity(table, which), NN
            )
            for which in range(2)
        )
        result[at, pl.ds(0, half)] = even + odd
        for j in range(tiles):
            lanes = slice(j * LANES, (j + 1) * LANES)
            result[at, pl.ds((2 * tiles - 1 - j) * LANES, LANES)] = reverse_lanes(
                even[:, lanes] - odd[:, lanes], LANES
            )
        copies.append(pltpu.make_async_copy(result.at[at, :], out.at[at, :], sem.at[i]))
        copies[-1].start()
    for copy in copies:
        copy.wait()


VMEM = pl.BlockSpec(memory_space=pltpu.VMEM)
HBM = pl.BlockSpec(memory_space=pltpu.HBM)


def shape(*dims, dtype=jnp.float32):
    return jax.ShapeDtypeStruct(dims, dtype)


def limit(mebibytes):
    return pltpu.CompilerParams(vmem_limit_bytes=mebibytes << 20)


def solution(mesh):
    slabs = mesh.shape["growth"]
    lat = mesh.shape["lat"]

    def per_device(source, spacing):
        slab, xlocal, width = source.shape
        devices = slabs * lat
        flat = slab * xlocal
        half = width // 2
        depth = slab * slabs
        table = jnp.asarray(half_table(width))
        eig = eigenvalues(width)
        eig_x = jnp.asarray(eig[None, :])
        eig_y = jnp.asarray(eig.reshape(devices, SUB).T)
        own = jnp.broadcast_to(spacing[:, None], (slab, LANES))
        others = [
            lax.ppermute(own, "growth", [((j + k) % slabs, j) for j in range(slabs)])
            for k in range(1, slabs)
        ]
        planes = pl.pallas_call(
            forward_y,
            out_shape=shape(width, flat),
            in_specs=[HBM, HBM],
            out_specs=HBM,
            scratch_shapes=[
                pltpu.VMEM((flat, width), jnp.float32),
                pltpu.VMEM((2 * width, half), jnp.bfloat16),
                pltpu.VMEM((width, flat), jnp.float32),
                pltpu.SemaphoreType.DMA,
                pltpu.SemaphoreType.DMA((4,)),
                pltpu.SemaphoreType.DMA((2,)),
            ],
            compiler_params=pltpu.CompilerParams(vmem_limit_bytes=67043328),
            name="forward_y",
        )(source.reshape(flat, width), table)
        moved = lax.all_to_all(planes.reshape(devices, SUB, flat), ALL, 0, 0, tiled=True)
        spatial = pl.pallas_call(
            middle,
            out_shape=shape(devices, SUB, flat),
            in_specs=[VMEM] * 8,
            out_specs=VMEM,
            scratch_shapes=[
                pltpu.VMEM((depth * SUB, width), jnp.float32),
                pltpu.VMEM((depth, LANES), jnp.float32),
                pltpu.VMEM((depth * SUB, width), jnp.float32),
            ],
            compiler_params=limit(24),
            name="middle",
        )(moved, table, own, *others, eig_x, eig_y)
        returned = lax.all_to_all(spatial, ALL, 0, 0, tiled=True)
        result = pl.pallas_call(
            inverse_y,
            out_shape=shape(flat, width),
            in_specs=[VMEM] * 2,
            out_specs=HBM,
            scratch_shapes=[
                pltpu.VMEM((flat, width), jnp.float32),
                pltpu.SemaphoreType.DMA((flat // LANES,)),
            ],
            compiler_params=limit(24),
            name="inverse_y",
        )(returned.reshape(width, flat), table)
        return result.reshape(slab, xlocal, width)

    return jax.shard_map(
        per_device,
        mesh=mesh,
        in_specs=(P("growth", "lat", None), P("growth")),
        out_specs=P("growth", "lat", None),
        check_vma=False,
    )
```

time: 75.5 us -> 64.3 us (0.85)
  local copies, waits for them, and re-layouts: 8.95 us -> 1.43 us
  Pallas kernels: 12.6 us -> 9.8 us
    unnamed x22 -> x6, local copies, waits for them, and re-layouts: 8.88 us -> 0.7 us
    pallas_call x1, Pallas kernels: 5.3 us -> 1.95 us  [per_device(): pl.pallas_call(inverse_y, out_shape=shape(flat, width), in_specs=[VMEM] *...]
    pallas_call x1, Pallas kernels: 3.09 us -> 4.76 us  [per_device(): pl.pallas_call(forward_y, out_shape=shape(width, flat), in_specs=[HBM, HB...]
    pallas_call x1, Pallas kernels: 4.21 us -> 3.09 us  [per_device(): pl.pallas_call(middle, out_shape=shape(devices, SUB, flat), in_specs=[VME...]
  transfers between devices with their start and end apart: 4 -> 4, of which waited for: 3 -> 3; matrix products, arithmetic and copies ran while one was open for 0% -> 1% of each run, Pallas kernels for 0% -> 0%
where the time goes in v1:
time: 64.3 us; the launch traced here: 64.1 us
  blocking collectives  23.3 us (36%)
  starting transfers between devices  15.6 us (24%)
  waiting for transfers between devices  13.9 us (22%)
  Pallas kernels  9.8 us (15%)
  local copies, waits for them, and re-layouts  1.43 us (2%)
    all_to_all x1, blocking collectives, per_device(): returned = lax.all_to_all(spatial, ALL, 0, 0, tiled=True)  23.3 us
    all_to_all x1, starting transfers between devices, per_device(): lax.all_to_all(planes.reshape(devices, SUB, flat), ALL, 0, 0, tiled=True)  11.5 us
    all_to_all x1, waiting for transfers between devices, per_device(): lax.all_to_all(planes.reshape(devices, SUB, flat), ALL, 0, 0, tiled=True)  10.3 us
    pallas_call x1, Pallas kernels, per_device(): pl.pallas_call(forward_y, out_shape=shape(width, flat), in_specs=[HBM, HB...  4.76 us
    ppermute x3, starting transfers between devices, per_device(): lax.ppermute(own, 'growth', [((j + k) % slabs, j) for j in range(slabs)])  4.12 us
    ppermute x3, waiting for transfers between devices, per_device(): lax.ppermute(own, 'growth', [((j + k) % slabs, j) for j in range(slabs)])  3.69 us
    pallas_call x1, Pallas kernels, per_device(): pl.pallas_call(middle, out_shape=shape(devices, SUB, flat), in_specs=[VME...  3.09 us
    pallas_call x1, Pallas kernels, per_device(): pl.pallas_call(inverse_y, out_shape=shape(flat, width), in_specs=[VMEM] *...  1.95 us
  transfers between devices with their start and end apart: 4, of which 3 were waited for; matrix products, arithmetic and copies ran while one was open for 1% of the time, Pallas kernels for 0%

profile of v1, /device:TPU:1, one launch (start us, length us, event | category | flops | bytes accessed | tf_op | source)
XLA Modules:
  0.0 64.1 jit_solution(15466802300972774864)
XLA Ops:
  0.0 4.8 %forward_y.1 = f32[1024,256]{1,0:T(8,128)} custom-call(f32[256,1024]{1,0:T(8,128)} %bitcast.6, bf16[2048,512]{1,0:T(8,128)(2,1)} %constant.6.clone.table_hbm.table), custom_call_target="tpu_custom_call" | custom-call | tf_op jit(solution)/shard_map/forward_y/pallas_call | solution.py:281
  4.8 0.0 copy-start
  4.8 0.0 copy-start.1
  4.8 11.5 %all-to-all-start = ((f32[128,8,256]{2,1,0:T(8,128)}), f32[128,8,256]{2,1,0:T(8,128)S(1)}, u32[]{:S(2)}, u32[]{:S(2)}) async-start(f32[128,8,256]{2,1,0:T(8,128)} %bitcast.5), calls=%async_computation | async-start | bytes 2097152 | tf_op jit(solution)/shard_map/all_to_all | solution.py:297
  16.3 0.7 %broadcast_in_dim.2.own = f32[8,128]{1,0:T(8,128)S(1)} broadcast(f32[8]{0:T(128)} %param.6), dimensions={0} | broadcast | bytes 4128 | tf_op jit(solution)/shard_map/broadcast_in_dim | solution.py:276
  17.0 3.2 %collective-permute-start = (f32[8,128]{1,0:T(8,128)S(1)}, f32[8,128]{1,0:T(8,128)S(1)}, u32[]{:S(2)}, u32[]{:S(2)}) collective-permute-start(f32[8,128]{1,0:T(8,128)S(1)} %broadcast_in_dim.2.own), channel_id=1, source_target_pairs={{32,0},{64,32},{96,64},{0,96},{33,1},{65,33},{97,65},{1,97},{34,2}... | collective-permute-start | bytes 12296 | tf_op jit(solution)/shard_map/ppermute | solution.py:278
  20.3 0.0 collective-permute-start.1
  20.3 0.8 %collective-permute-start.2 = (f32[8,128]{1,0:T(8,128)S(1)}, f32[8,128]{1,0:T(8,128)S(1)}, u32[]{:S(2)}, u32[]{:S(2)}) collective-permute-start(f32[8,128]{1,0:T(8,128)S(1)} %broadcast_in_dim.2.own), channel_id=1, source_target_pairs={{96,0},{0,32},{32,64},{64,96},{97,1},{1,33},{33,65},{65,97},{98,2}... | collective-permute-start | bytes 12296 | tf_op jit(solution)/shard_map/ppermute | solution.py:278
  21.1 0.0 collective-permute-done.next1
  21.1 3.6 %collective-permute-done.1.next2 = f32[8,128]{1,0:T(8,128)S(1)} collective-permute-done((f32[8,128]{1,0:T(8,128)S(1)}, f32[8,128]{1,0:T(8,128)S(1)}, u32[]{:S(2)}, u32[]{:S(2)}) %collective-permute-start.1) | collective-permute-done | bytes 4128 | tf_op jit(solution)/shard_map/ppermute | solution.py:278
  24.8 0.1 collective-permute-done.2.next3
  24.8 10.3 %all-to-all-done.moved = f32[128,8,256]{2,1,0:T(8,128)S(1)} async-done(((f32[128,8,256]{2,1,0:T(8,128)}), f32[128,8,256]{2,1,0:T(8,128)S(1)}, u32[]{:S(2)}, u32[]{:S(2)}) %all-to-all-start) | async-done | bytes 1048608 | tf_op jit(solution)/shard_map/all_to_all | solution.py:297
  35.1 0.0 copy-done
  35.1 0.0 copy-done.1
  35.1 0.0 copy-start.2
  35.1 0.7 %copy-done.2 = f32[8,128]{1,0:T(8,128)S(1)} copy-done((f32[8,128]{1,0:T(8,128)S(1)}, f32[8,128]{1,0:T(8,128)}, u32[]{:S(2)}) %copy-start.2) | copy-done | bytes 4120
  35.8 3.1 %middle.1 = f32[128,8,256]{2,1,0:T(8,128)S(1)} custom-call(f32[128,8,256]{2,1,0:T(8,128)S(1)} %all-to-all-done.moved, bf16[2048,512]{1,0:T(8,128)(2,1)S(1)} %copy-done, f32[8,128]{1,0:T(8,128)S(1)} %broadcast_in_dim.2.own, f32[8,128]{1,0:T(8,128)S(1)} %collective-permute-done.next1, f32[8,128]{1,0:T(8,128)S(1)} %collective-permute-done.1.next2, ...), custom_call_target="tpu_custom_call" | custom-call | tf_op jit(solution)/shard_map/middle/pallas_call | solution.py:298
  38.9 23.3 %all_to_all.10 = f32[128,8,256]{2,1,0:T(8,128)S(1)} all-to-all(f32[128,8,256]{2,1,0:T(8,128)S(1)} %middle.1), channel_id=1, replica_groups=mesh['growth'=4,'lat'=32] {'growth','lat'}, dimensions={0} | all-to-all | bytes 2097152 | tf_op jit(solution)/shard_map/all_to_all | solution.py:311
  62.1 2.0 %inverse_y.1 = f32[256,1024]{1,0:T(8,128)} custom-call(f32[1024,256]{1,0:T(8,128)S(1)} %bitcast.4, bf16[2048,512]{1,0:T(8,128)(2,1)S(1)} %copy-done), custom_call_target="tpu_custom_call" | custom-call | tf_op jit(solution)/shard_map/inverse_y/pallas_call | solution.py:312
Async XLA Ops:
  4.8 30.3 %copy-start = (bf16[2048,512]{1,0:T(8,128)(2,1)S(1)}, bf16[2048,512]{1,0:T(8,128)(2,1)}, u32[]{:S(2)}) copy-start(bf16[2048,512]{1,0:T(8,128)(2,1)} %constant.6.clone.table_hbm.table) | copy-start | bytes 6291460
  4.8 30.3 %copy-start.1 = (f32[1,1024]{1,0:T(1,128)S(1)}, f32[1,1024]{1,0:T(1,128)}, u32[]{:S(2)}) copy-start(f32[1,1024]{1,0:T(1,128)} %constant.7.clone.eig_x) | copy-start | bytes 12292
  4.8 30.3 %all-to-all-start = ((f32[128,8,256]{2,1,0:T(8,128)}), f32[128,8,256]{2,1,0:T(8,128)S(1)}, u32[]{:S(2)}, u32[]{:S(2)}) async-start(f32[128,8,256]{2,1,0:T(8,128)} %bitcast.5), calls=%async_computation | async-start | bytes 2097152 | tf_op jit(solution)/shard_map/all_to_all | solution.py:297
  17.0 4.1 %collective-permute-start = (f32[8,128]{1,0:T(8,128)S(1)}, f32[8,128]{1,0:T(8,128)S(1)}, u32[]{:S(2)}, u32[]{:S(2)}) collective-permute-start(f32[8,128]{1,0:T(8,128)S(1)} %broadcast_in_dim.2.own), channel_id=1, source_target_pairs={{32,0},{64,32},{96,64},{0,96},{33,1},{65,33},{97,65},{1,97},{34,2}... | collective-permute-start | bytes 12296 | tf_op jit(solution)/shard_map/ppermute | solution.py:278
  20.3 4.5 %collective-permute-start.1 = (f32[8,128]{1,0:T(8,128)S(1)}, f32[8,128]{1,0:T(8,128)S(1)}, u32[]{:S(2)}, u32[]{:S(2)}) collective-permute-start(f32[8,128]{1,0:T(8,128)S(1)} %broadcast_in_dim.2.own), channel_id=1, source_target_pairs={{64,0},{96,32},{0,64},{32,96},{65,1},{97,33},{1,65},{33,97},{66,2}... | collective-permute-start | bytes 12296 | tf_op jit(solution)/shard_map/ppermute | solution.py:278
  20.3 4.5 %collective-permute-start.2 = (f32[8,128]{1,0:T(8,128)S(1)}, f32[8,128]{1,0:T(8,128)S(1)}, u32[]{:S(2)}, u32[]{:S(2)}) collective-permute-start(f32[8,128]{1,0:T(8,128)S(1)} %broadcast_in_dim.2.own), channel_id=1, source_target_pairs={{96,0},{0,32},{32,64},{64,96},{97,1},{1,33},{33,65},{65,97},{98,2}... | collective-permute-start | bytes 12296 | tf_op jit(solution)/shard_map/ppermute | solution.py:278
  35.1 0.7 %copy-start.2 = (f32[8,128]{1,0:T(8,128)S(1)}, f32[8,128]{1,0:T(8,128)}, u32[]{:S(2)}) copy-start(f32[8,128]{1,0:T(8,128)} %constant.8.clone.eig_y) | copy-start | bytes 12292

commit v2 on v1

v2 whole, which is shorter than its diff:
```python
import math

import jax
import jax.numpy as jnp
import numpy as np
from jax import lax
from jax.experimental import pallas as pl
from jax.experimental.pallas import tpu as pltpu
from jax.sharding import PartitionSpec as P

ALL = ("growth", "lat")
LANES = 128
SUB = 8
GROUP = 32
NT = ((1,), (1,))
NN = ((1,), (0,))


def mode_order(points):
    return np.concatenate([np.arange(0, points, 2), np.arange(1, points, 2)])


def half_table(points):
    k = mode_order(points)[:, None].astype(np.int64)
    j = np.arange(points // 2, dtype=np.int64)[None, :]
    angle = ((2 * j + 1) * k % (4 * points)).astype(np.float64) * (math.pi / (2.0 * points))
    scale = np.where(k == 0, math.sqrt(1.0 / points), math.sqrt(2.0 / points))
    table = (scale * np.cos(angle)).astype(np.float32)
    high = table.astype(jnp.bfloat16)
    low = (table - high.astype(np.float32)).astype(jnp.bfloat16)
    return np.concatenate([high, low], axis=0)


def quarter_sine(angle):
    square = angle * angle
    value = 1.0 - square * (1.0 / 156.0)
    for divisor in (110.0, 72.0, 42.0, 20.0, 6.0):
        value = 1.0 - square * value * (1.0 / divisor)
    return angle * value


def eigenvalue(slot, points):
    half = points // 2
    mode = jnp.where(slot < half, 2 * slot, 2 * (slot - half) + 1)
    sine = quarter_sine(mode.astype(jnp.float32) * (math.pi / (2.0 * points)))
    return 4.0 * sine * sine


def split(value):
    high = value.astype(jnp.bfloat16)
    low = (value - high.astype(jnp.float32)).astype(jnp.bfloat16)
    return high, low


def product(left, right, dims):
    def one(a, b):
        return lax.dot_general(a, b, (dims, ((), ())), preferred_element_type=jnp.float32)

    return one(left[0], right[0]) + (one(left[0], right[1]) + one(left[1], right[0]))


def shared(left, right, dims):
    def one(a, b):
        return lax.dot_general(a, b, (dims, ((), ())), preferred_element_type=jnp.float32)

    count = left[0].shape[0]
    both = one(jnp.concatenate(left, axis=0), right[0])
    return both[:count] + (one(left[0], right[1]) + both[count:])


def parity(table, which):
    n = table.shape[0] // 4
    return (
        table[which * n : (which + 1) * n, :],
        table[(2 + which) * n : (3 + which) * n, :],
    )


def reverse_lanes(value, span):
    lane = lax.broadcasted_iota(jnp.int32, value.shape, 1)
    source = lane // span * span + (span - 1) - lane % span
    return jnp.take_along_axis(value, source, axis=1)


def forward_y(source, table_hbm, out_hbm, rows, table, out, sem, table_sem, out_sem):
    flat, points = rows.shape
    half = points // 2
    tiles = half // LANES
    pieces = 4
    step = points // pieces
    fetch = pltpu.make_async_copy(source, rows, sem)
    fetch.start()

    def table_copy(i):
        at = pl.ds(pl.multiple_of((i % 2) * points + (i // 2) * half, half), half)
        return pltpu.make_async_copy(table_hbm.at[at, :], table.at[at, :], table_sem.at[i])

    @pl.loop(0, 4)
    def _(i):
        table_copy(i).start()

    fetch.wait()
    first = [rows[:, pl.ds(j * LANES, LANES)] for j in range(tiles)]
    second = [
        reverse_lanes(rows[:, pl.ds((2 * tiles - 1 - j) * LANES, LANES)], LANES)
        for j in range(tiles)
    ]
    folded = (
        split(jnp.concatenate([a + b for a, b in zip(first, second)], axis=1)),
        split(jnp.concatenate([a - b for a, b in zip(first, second)], axis=1)),
    )
    copies = []
    for i in range(pieces):
        which = i * 2 // pieces
        if i % (pieces // 2) == 0:
            table_copy(2 * which).wait()
            table_copy(2 * which + 1).wait()
        at = pl.ds(i * step, step)
        low = pl.ds(points + i * step, step)
        out[at, :] = product((table[at, :], table[low, :]), folded[which], NT)
        copies.append(pltpu.make_async_copy(out.at[at, :], out_hbm.at[at, :], out_sem.at[i]))
        copies[-1].start()
    for copy in copies:
        copy.wait()


def permute(value, source):
    return jnp.take_along_axis(value, source, axis=1)


def exchange(a, b, keep, source, turn=None):
    moved = permute(jnp.where(keep, b, a), source)
    if turn is None:
        return jnp.where(keep, a, moved), jnp.where(keep, moved, b)
    kept = permute(jnp.where(keep, a, b), turn)
    return jnp.where(keep, kept, moved), jnp.where(keep, moved, kept)


def swap_groups(v, lane, reverse):
    keep = lane < 2 * GROUP
    t0, t2 = exchange(v[0], v[2], keep, lane ^ (2 * GROUP))
    t1, t3 = exchange(v[1], v[3], keep, lane ^ (2 * GROUP))
    keep = lane // GROUP % 2 == 0
    source, turn = lane ^ GROUP, None
    if reverse:
        source, turn = lane ^ (2 * GROUP - 1), lane ^ (GROUP - 1)
    w0, w1 = exchange(t0, t1, keep, source, turn)
    w2, w3 = exchange(t2, t3, keep, source, turn)
    return w0, w1, w2, w3


def wide(row, width):
    return jnp.concatenate([jnp.broadcast_to(row, (SUB, LANES))] * (width // LANES), axis=1)


def conductances(h):
    zero = jnp.zeros_like(h[0])
    padded = [zero] + h + [zero]
    return [2.0 / (padded[i] + padded[i + 1]) for i in range(len(h) + 1)]


def pivots(own, next1, next2, next3, heights, inverse):
    slab = own.shape[0]
    slabs = 4
    depth = slab * slabs
    width = inverse.shape[1]
    grow = lax.axis_index("growth")
    rank = grow * lax.axis_size("lat") + lax.axis_index("lat")
    for k, ref in enumerate((own, next1, next2, next3)):
        at = pl.ds(pl.multiple_of(lax.rem(grow + k, slabs) * slab, slab), slab)
        heights[at, :] = ref[...]
    row = lax.broadcasted_iota(jnp.int32, (SUB, LANES), 0) + rank * SUB
    column = lax.broadcasted_iota(jnp.int32, (SUB, width), 1)
    ey = jnp.concatenate([eigenvalue(row, width)] * (width // LANES), axis=1)
    total = ey + eigenvalue(column, width)
    h = [heights[z : z + 1, :] for z in range(depth)]
    conduct = conductances(h)
    inv = None
    for z in range(depth):
        pivot = wide(conduct[z] + conduct[z + 1], width) + wide(h[z], width) * total
        if z:
            pivot = pivot - wide(conduct[z] * conduct[z], width) * inv
        inv = 1.0 / pivot
        inverse[pl.ds(z * SUB, SUB), :] = inv


def middle(
    moved, table, own, next1, next2, next3, out, rows, heights, inverse
):
    slabs = 4
    pivots(own, next1, next2, next3, heights, inverse)
    depth = heights.shape[0]
    slab = depth // slabs
    lat = moved.shape[0] // slabs
    width = rows.shape[1]
    half = width // 2
    tiles = half // LANES
    lane = lax.broadcasted_iota(jnp.int32, (SUB, LANES), 1)
    chunks = 2
    span = half // chunks
    blocks = [(g, s) for g in range(slabs) for s in range(2)]

    def part(which, high):
        return pl.ds((0 if high else width) + which * half, half)

    sums = [None, None]
    for c in range(chunks):
        for g, s in blocks:
            lanes = pl.ds(s * LANES, LANES)
            for j in range(c * tiles // chunks, (c + 1) * tiles // chunks):
                first = swap_groups(
                    [moved[g * lat + 4 * j + i, :, lanes] for i in range(4)], lane, False
                )
                second = swap_groups(
                    [moved[g * lat + lat - 1 - 4 * j - i, :, lanes] for i in range(4)],
                    lane,
                    True,
                )
                for q in range(4):
                    at = pl.ds((g * slab + s * 4 + q) * SUB, SUB)
                    rows[at, pl.ds(j * LANES, LANES)] = first[q] + second[q]
                    rows[at, pl.ds(half + j * LANES, LANES)] = first[q] - second[q]
        at = pl.ds(c * span, span)
        for which in range(2):
            data = split(rows[:, pl.ds(which * half + c * span, span)])
            value = shared(data, (table[part(which, 1), at], table[part(which, 0), at]), NT)
            sums[which] = value if c == 0 else sums[which] + value

    h = [heights[z : z + 1, :] for z in range(depth)]
    conduct = conductances(h)

    def solve(which):
        lanes = pl.ds(which * half, half)
        partial = None
        for z in range(depth):
            at = pl.ds(z * SUB, SUB)
            value = wide(h[z], half) * rows[at, lanes]
            if z:
                value = value + wide(conduct[z], half) * partial
            partial = value * inverse[at, lanes]
            rows[at, lanes] = partial
        solved = partial
        for z in reversed(range(depth - 1)):
            at = pl.ds(z * SUB, SUB)
            solved = rows[at, lanes] + wide(conduct[z + 1], half) * inverse[at, lanes] * solved
            rows[at, lanes] = solved

    data = []
    for which in range(2):
        rows[:, pl.ds(which * half, half)] = sums[which]
    for which in range(2):
        solve(which)
        data.append(split(rows[:, pl.ds(which * half, half)]))
    for c in range(chunks):
        at = pl.ds(c * span, span)
        even, odd = (
            shared(data[which], (table[part(which, 1), at], table[part(which, 0), at]), NN)
            for which in range(2)
        )
        total, rest = even + odd, even - odd
        for g, s in blocks:
            lanes = pl.ds(s * LANES, LANES)
            for j in range(tiles // chunks):
                where = [
                    slice((g * slab + s * 4 + q) * SUB, (g * slab + s * 4 + q + 1) * SUB)
                    for q in range(4)
                ]
                cols = slice(j * LANES, (j + 1) * LANES)
                base = 4 * (c * tiles // chunks + j)
                for i, v in enumerate(swap_groups([total[w, cols] for w in where], lane, False)):
                    out[g * lat + base + i, :, lanes] = v
                for i, v in enumerate(swap_groups([rest[w, cols] for w in where], lane, True)):
                    out[g * lat + lat - 1 - base - i, :, lanes] = v


def inverse_y(planes, table, out, result, sem):
    points = planes.shape[0]
    half = points // 2
    chunks = 2
    span = half // chunks
    tiles = span // LANES
    data = [split(planes[pl.ds(which * half, half), :].T) for which in range(2)]
    copies = []

    def send(at):
        copies.append(
            pltpu.make_async_copy(result.at[:, at], out.at[:, at], sem.at[len(copies)])
        )
        copies[-1].start()

    for c in range(chunks):
        at = pl.ds(c * span, span)
        even, odd = (
            shared(
                data[which],
                (
                    table[pl.ds(which * half, half), at],
                    table[pl.ds(points + which * half, half), at],
                ),
                NN,
            )
            for which in range(2)
        )
        result[:, at] = even + odd
        send(at)
        rest = even - odd
        mirror = points - (c + 1) * span
        for j in range(tiles):
            lanes = slice((tiles - 1 - j) * LANES, (tiles - j) * LANES)
            result[:, pl.ds(mirror + j * LANES, LANES)] = reverse_lanes(rest[:, lanes], LANES)
        send(pl.ds(mirror, span))
    for copy in copies:
        copy.wait()


VMEM = pl.BlockSpec(memory_space=pltpu.VMEM)
HBM = pl.BlockSpec(memory_space=pltpu.HBM)


def shape(*dims, dtype=jnp.float32):
    return jax.ShapeDtypeStruct(dims, dtype)


FULL = 67043328


def limit(size):
    return pltpu.CompilerParams(vmem_limit_bytes=size)


def solution(mesh):
    slabs = mesh.shape["growth"]
    lat = mesh.shape["lat"]

    def per_device(source, spacing):
        slab, xlocal, width = source.shape
        devices = slabs * lat
        flat = slab * xlocal
        half = width // 2
        depth = slab * slabs
        table = jnp.asarray(half_table(width))
        own = jnp.broadcast_to(spacing[:, None], (slab, LANES))
        others = [
            lax.ppermute(own, "growth", [((j + k) % slabs, j) for j in range(slabs)])
            for k in range(1, slabs)
        ]
        planes = pl.pallas_call(
            forward_y,
            out_shape=shape(width, flat),
            in_specs=[HBM, HBM],
            out_specs=HBM,
            scratch_shapes=[
                pltpu.VMEM((flat, width), jnp.float32),
                pltpu.VMEM((2 * width, half), jnp.bfloat16),
                pltpu.VMEM((width, flat), jnp.float32),
                pltpu.SemaphoreType.DMA,
                pltpu.SemaphoreType.DMA((4,)),
                pltpu.SemaphoreType.DMA((4,)),
            ],
            compiler_params=limit(FULL),
            name="forward_y",
        )(source.reshape(flat, width), table)
        moved = lax.all_to_all(planes.reshape(devices, SUB, flat), ALL, 0, 0, tiled=True)
        spatial = pl.pallas_call(
            middle,
            out_shape=shape(devices, SUB, flat),
            in_specs=[VMEM] * 6,
            out_specs=VMEM,
            scratch_shapes=[
                pltpu.VMEM((depth * SUB, width), jnp.float32),
                pltpu.VMEM((depth, LANES), jnp.float32),
                pltpu.VMEM((depth * SUB, width), jnp.float32),
            ],
            compiler_params=limit(24 << 20),
            name="middle",
        )(moved, table, own, *others)
        returned = lax.all_to_all(spatial, ALL, 0, 0, tiled=True)
        result = pl.pallas_call(
            inverse_y,
            out_shape=shape(flat, width),
            in_specs=[VMEM] * 2,
            out_specs=HBM,
            scratch_shapes=[
                pltpu.VMEM((flat, width), jnp.float32),
                pltpu.SemaphoreType.DMA((4,)),
            ],
            compiler_params=limit(24 << 20),
            name="inverse_y",
        )(returned.reshape(width, flat), table)
        return result.reshape(slab, xlocal, width)

    return jax.shard_map(
        per_device,
        mesh=mesh,
        in_specs=(P("growth", "lat", None), P("growth")),
        out_specs=P("growth", "lat", None),
        check_vma=False,
    )
```

time: 64.3 us -> 62.1 us (0.966)
  Pallas kernels: 9.8 us -> 8.28 us
  local copies, waits for them, and re-layouts: 1.43 us -> 0.08 us
  waiting for transfers between devices: 13.9 us -> 14.6 us
    pallas_call x1, Pallas kernels: 4.76 us -> 3.6 us  [per_device(): pl.pallas_call(forward_y, out_shape=shape(width, flat), in_specs=[HBM, HB...]
    unnamed x6 -> x4, local copies, waits for them, and re-layouts: 0.7 us -> 0.01 us
    broadcast_in_dim x1, local copies, waits for them, and re-layouts: 0.73 us -> 0.07 us  [per_device(): own = jnp.broadcast_to(spacing[:, None], (slab, LANES))]
  transfers between devices with their start and end apart: 4 -> 4, of which waited for: 3 -> 3; matrix products, arithmetic and copies ran while one was open for 1% -> 0% of each run, Pallas kernels for 0% -> 0%
where the time goes in v2:
time: 62.1 us; the launch traced here: 61.9 us
  blocking collectives  23.3 us (38%)
  starting transfers between devices  15.6 us (25%)
  waiting for transfers between devices  14.6 us (24%)
  Pallas kernels  8.28 us (13%)
    all_to_all x1, blocking collectives, per_device(): returned = lax.all_to_all(spatial, ALL, 0, 0, tiled=True)  23.3 us
    all_to_all x1, starting transfers between devices, per_device(): lax.all_to_all(planes.reshape(devices, SUB, flat), ALL, 0, 0, tiled=True)  11.5 us
    all_to_all x1, waiting for transfers between devices, per_device(): lax.all_to_all(planes.reshape(devices, SUB, flat), ALL, 0, 0, tiled=True)  10.3 us
    ppermute x3, waiting for transfers between devices, per_device(): lax.ppermute(own, 'growth', [((j + k) % slabs, j) for j in range(slabs)])  4.32 us
    ppermute x3, starting transfers between devices, per_device(): lax.ppermute(own, 'growth', [((j + k) % slabs, j) for j in range(slabs)])  4.13 us
    pallas_call x1, Pallas kernels, per_device(): pl.pallas_call(forward_y, out_shape=shape(width, flat), in_specs=[HBM, HB...  3.6 us
    pallas_call x1, Pallas kernels, per_device(): pl.pallas_call(middle, out_shape=shape(devices, SUB, flat), in_specs=[VME...  2.74 us
    pallas_call x1, Pallas kernels, per_device(): pl.pallas_call(inverse_y, out_shape=shape(flat, width), in_specs=[VMEM] *...  1.93 us
  transfers between devices with their start and end apart: 4, of which 3 were waited for; matrix products, arithmetic and copies ran while one was open for 0% of the time, Pallas kernels for 0%

profile of v2, /device:TPU:1, one launch (start us, length us, event | category | flops | bytes accessed | tf_op | source)
XLA Modules:
  0.0 61.9 jit_solution(14851981406797790190)
XLA Ops:
  0.0 3.6 %forward_y.1 = f32[1024,256]{1,0:T(8,128)} custom-call(f32[256,1024]{1,0:T(8,128)} %bitcast.6, bf16[2048,512]{1,0:T(8,128)(2,1)} %constant.2.clone.table_hbm.table), custom_call_target="tpu_custom_call" | custom-call | tf_op jit(solution)/shard_map/forward_y/pallas_call | solution.py:347
  3.6 0.0 copy-start.1
  3.6 0.0 copy-start
  3.6 11.5 %all-to-all-start = ((f32[128,8,256]{2,1,0:T(8,128)}), f32[128,8,256]{2,1,0:T(8,128)S(1)}, u32[]{:S(2)}, u32[]{:S(2)}) async-start(f32[128,8,256]{2,1,0:T(8,128)} %bitcast.5), calls=%async_computation | async-start | bytes 2097152 | tf_op jit(solution)/shard_map/all_to_all | solution.py:363
  15.1 0.0 copy-done.1
  15.1 0.1 broadcast_in_dim.2.own
  15.2 3.2 %collective-permute-start = (f32[8,128]{1,0:T(8,128)S(1)}, f32[8,128]{1,0:T(8,128)S(1)}, u32[]{:S(2)}, u32[]{:S(2)}) collective-permute-start(f32[8,128]{1,0:T(8,128)S(1)} %broadcast_in_dim.2.own), channel_id=1, source_target_pairs={{32,0},{64,32},{96,64},{0,96},{33,1},{65,33},{97,65},{1,97},{34,2}... | collective-permute-start | bytes 12296 | tf_op jit(solution)/shard_map/ppermute | solution.py:344
  18.5 0.1 collective-permute-start.1
  18.6 0.8 %collective-permute-start.2 = (f32[8,128]{1,0:T(8,128)S(1)}, f32[8,128]{1,0:T(8,128)S(1)}, u32[]{:S(2)}, u32[]{:S(2)}) collective-permute-start(f32[8,128]{1,0:T(8,128)S(1)} %broadcast_in_dim.2.own), channel_id=1, source_target_pairs={{96,0},{0,32},{32,64},{64,96},{97,1},{1,33},{33,65},{65,97},{98,2}... | collective-permute-start | bytes 12296 | tf_op jit(solution)/shard_map/ppermute | solution.py:344
  19.3 0.0 collective-permute-done.next1
  19.4 4.3 %collective-permute-done.1.next2 = f32[8,128]{1,0:T(8,128)S(1)} collective-permute-done((f32[8,128]{1,0:T(8,128)S(1)}, f32[8,128]{1,0:T(8,128)S(1)}, u32[]{:S(2)}, u32[]{:S(2)}) %collective-permute-start.1) | collective-permute-done | bytes 4128 | tf_op jit(solution)/shard_map/ppermute | solution.py:344
  23.6 0.1 collective-permute-done.2.next3
  23.7 10.3 %all-to-all-done.moved = f32[128,8,256]{2,1,0:T(8,128)S(1)} async-done(((f32[128,8,256]{2,1,0:T(8,128)}), f32[128,8,256]{2,1,0:T(8,128)S(1)}, u32[]{:S(2)}, u32[]{:S(2)}) %all-to-all-start) | async-done | bytes 1048608 | tf_op jit(solution)/shard_map/all_to_all | solution.py:363
  33.9 0.0 copy-done
  33.9 2.7 %middle.1 = f32[128,8,256]{2,1,0:T(8,128)S(1)} custom-call(f32[128,8,256]{2,1,0:T(8,128)S(1)} %all-to-all-done.moved, bf16[2048,512]{1,0:T(8,128)(2,1)S(1)} %copy-done, f32[8,128]{1,0:T(8,128)S(1)} %broadcast_in_dim.2.own, f32[8,128]{1,0:T(8,128)S(1)} %collective-permute-done.next1, f32[8,128]{1,0:T(8,128)S(1)} %collective-permute-done.1.next2, ...), custom_call_target="tpu_custom_call" | custom-call | tf_op jit(solution)/shard_map/middle/pallas_call | solution.py:364
  36.7 23.3 %all_to_all.10 = f32[128,8,256]{2,1,0:T(8,128)S(1)} all-to-all(f32[128,8,256]{2,1,0:T(8,128)S(1)} %middle.1), channel_id=1, replica_groups=mesh['growth'=4,'lat'=32] {'growth','lat'}, dimensions={0} | all-to-all | bytes 2097152 | tf_op jit(solution)/shard_map/all_to_all | solution.py:377
  59.9 1.9 %inverse_y.1 = f32[256,1024]{1,0:T(8,128)} custom-call(f32[1024,256]{1,0:T(8,128)S(1)} %bitcast.4, bf16[2048,512]{1,0:T(8,128)(2,1)S(1)} %copy-done), custom_call_target="tpu_custom_call" | custom-call | tf_op jit(solution)/shard_map/inverse_y/pallas_call | solution.py:378
Async XLA Ops:
  3.6 11.5 %copy-start.1 = (f32[8]{0:T(128)S(1)}, f32[8]{0:T(128)}, u32[]{:S(2)}) copy-start(f32[8]{0:T(128)} %param.4) | copy-start | bytes 100
  3.6 30.3 %copy-start = (bf16[2048,512]{1,0:T(8,128)(2,1)S(1)}, bf16[2048,512]{1,0:T(8,128)(2,1)}, u32[]{:S(2)}) copy-start(bf16[2048,512]{1,0:T(8,128)(2,1)} %constant.2.clone.table_hbm.table) | copy-start | bytes 6291460
  3.6 30.3 %all-to-all-start = ((f32[128,8,256]{2,1,0:T(8,128)}), f32[128,8,256]{2,1,0:T(8,128)S(1)}, u32[]{:S(2)}, u32[]{:S(2)}) async-start(f32[128,8,256]{2,1,0:T(8,128)} %bitcast.5), calls=%async_computation | async-start | bytes 2097152 | tf_op jit(solution)/shard_map/all_to_all | solution.py:363
  15.2 4.1 %collective-permute-start = (f32[8,128]{1,0:T(8,128)S(1)}, f32[8,128]{1,0:T(8,128)S(1)}, u32[]{:S(2)}, u32[]{:S(2)}) collective-permute-start(f32[8,128]{1,0:T(8,128)S(1)} %broadcast_in_dim.2.own), channel_id=1, source_target_pairs={{32,0},{64,32},{96,64},{0,96},{33,1},{65,33},{97,65},{1,97},{34,2}... | collective-permute-start | bytes 12296 | tf_op jit(solution)/shard_map/ppermute | solution.py:344
  18.5 5.2 %collective-permute-start.1 = (f32[8,128]{1,0:T(8,128)S(1)}, f32[8,128]{1,0:T(8,128)S(1)}, u32[]{:S(2)}, u32[]{:S(2)}) collective-permute-start(f32[8,128]{1,0:T(8,128)S(1)} %broadcast_in_dim.2.own), channel_id=1, source_target_pairs={{64,0},{96,32},{0,64},{32,96},{65,1},{97,33},{1,65},{33,97},{66,2}... | collective-permute-start | bytes 12296 | tf_op jit(solution)/shard_map/ppermute | solution.py:344
  18.6 5.1 %collective-permute-start.2 = (f32[8,128]{1,0:T(8,128)S(1)}, f32[8,128]{1,0:T(8,128)S(1)}, u32[]{:S(2)}, u32[]{:S(2)}) collective-permute-start(f32[8,128]{1,0:T(8,128)S(1)} %broadcast_in_dim.2.own), channel_id=1, source_target_pairs={{96,0},{0,32},{32,64},{64,96},{97,1},{1,33},{33,65},{65,97},{98,2}... | collective-permute-start | bytes 12296 | tf_op jit(solution)/shard_map/ppermute | solution.py:344

commit v3 on v2

--- a/solution.py
+++ b/solution.py
@@ -129,7 +129,8 @@
 
 
 def exchange(a, b, keep, source, turn=None):
-    moved = permute(jnp.where(keep, b, a), source)
+    moved = jnp.where(keep, b, a)
+    moved = pltpu.roll(moved, LANES // 2, 1) if source is None else permute(moved, source)
     if turn is None:
         return jnp.where(keep, a, moved), jnp.where(keep, moved, b)
     kept = permute(jnp.where(keep, a, b), turn)
@@ -138,15 +139,13 @@
 
 def swap_groups(v, lane, reverse):
     keep = lane < 2 * GROUP
-    t0, t2 = exchange(v[0], v[2], keep, lane ^ (2 * GROUP))
-    t1, t3 = exchange(v[1], v[3], keep, lane ^ (2 * GROUP))
+    t0, t2 = exchange(v[0], v[2], keep, None)
+    t1, t3 = exchange(v[1], v[3], keep, None)
     keep = lane // GROUP % 2 == 0
-    source, turn = lane ^ GROUP, None
+    w = exchange(t0, t1, keep, lane ^ GROUP) + exchange(t2, t3, keep, lane ^ GROUP)
     if reverse:
-        source, turn = lane ^ (2 * GROUP - 1), lane ^ (GROUP - 1)
-    w0, w1 = exchange(t0, t1, keep, source, turn)
-    w2, w3 = exchange(t2, t3, keep, source, turn)
-    return w0, w1, w2, w3
+        w = tuple(permute(x, lane ^ (GROUP - 1)) for x in w)
+    return w
 
 
 def wide(row, width):
@@ -185,7 +184,7 @@
 
 
 def middle(
-    moved, table, own, next1, next2, next3, out, rows, heights, inverse
+    moved, table, own, next1, next2, next3, out, rows, modal, heights, inverse
 ):
     slabs = 4
     pivots(own, next1, next2, next3, heights, inverse)
@@ -203,7 +202,6 @@
     def part(which, high):
         return pl.ds((0 if high else width) + which * half, half)
 
-    sums = [None, None]
     for c in range(chunks):
         for g, s in blocks:
             lanes = pl.ds(s * LANES, LANES)
@@ -224,7 +222,8 @@
         for which in range(2):
             data = split(rows[:, pl.ds(which * half + c * span, span)])
             value = shared(data, (table[part(which, 1), at], table[part(which, 0), at]), NT)
-            sums[which] = value if c == 0 else sums[which] + value
+            to = pl.ds(which * half, half)
+            modal[:, to] = value if c == 0 else modal[:, to] + value
 
     h = [heights[z : z + 1, :] for z in range(depth)]
     conduct = conductances(h)
@@ -234,43 +233,46 @@
         partial = None
         for z in range(depth):
             at = pl.ds(z * SUB, SUB)
-            value = wide(h[z], half) * rows[at, lanes]
+            value = wide(h[z], half) * modal[at, lanes]
             if z:
                 value = value + wide(conduct[z], half) * partial
             partial = value * inverse[at, lanes]
-            rows[at, lanes] = partial
+            modal[at, lanes] = partial
         solved = partial
         for z in reversed(range(depth - 1)):
             at = pl.ds(z * SUB, SUB)
-            solved = rows[at, lanes] + wide(conduct[z + 1], half) * inverse[at, lanes] * solved
-            rows[at, lanes] = solved
-
-    data = []
-    for which in range(2):
-        rows[:, pl.ds(which * half, half)] = sums[which]
-    for which in range(2):
-        solve(which)
-        data.append(split(rows[:, pl.ds(which * half, half)]))
+            solved = modal[at, lanes] + wide(conduct[z + 1], half) * inverse[at, lanes] * solved
+            modal[at, lanes] = solved
+
+    def inverse_x(which, data, c):
+        at = pl.ds(c * span, span)
+        rows[:, pl.ds(which * half + c * span, span)] = shared(
+            data, (table[part(which, 1), at], table[part(which, 0), at]), NN
+        )
+
+    solve(0)
+    even = split(modal[:, pl.ds(0, half)])
     for c in range(chunks):
-        at = pl.ds(c * span, span)
-        even, odd = (
-            shared(data[which], (table[part(which, 1), at], table[part(which, 0), at]), NN)
-            for which in range(2)
-        )
-        total, rest = even + odd, even - odd
+        inverse_x(0, even, c)
+    solve(1)
+    odd = split(modal[:, pl.ds(half, half)])
+    for c in range(chunks):
+        inverse_x(1, odd, c)
         for g, s in blocks:
             lanes = pl.ds(s * LANES, LANES)
-            for j in range(tiles // chunks):
-                where = [
-                    slice((g * slab + s * 4 + q) * SUB, (g * slab + s * 4 + q + 1) * SUB)
-                    for q in range(4)
-                ]
-                cols = slice(j * LANES, (j + 1) * LANES)
-                base = 4 * (c * tiles // chunks + j)
-                for i, v in enumerate(swap_groups([total[w, cols] for w in where], lane, False)):
-                    out[g * lat + base + i, :, lanes] = v
-                for i, v in enumerate(swap_groups([rest[w, cols] for w in where], lane, True)):
-                    out[g * lat + lat - 1 - base - i, :, lanes] = v
+            for j in range(c * tiles // chunks, (c + 1) * tiles // chunks):
+                first = []
+                second = []
+                for q in range(4):
+                    where = pl.ds((g * slab + s * 4 + q) * SUB, SUB)
+                    a = rows[where, pl.ds(j * LANES, LANES)]
+                    b = rows[where, pl.ds(half + j * LANES, LANES)]
+                    first.append(a + b)
+                    second.append(a - b)
+                for i, v in enumerate(swap_groups(first, lane, False)):
+                    out[g * lat + 4 * j + i, :, lanes] = v
+                for i, v in enumerate(swap_groups(second, lane, True)):
+                    out[g * lat + lat - 1 - 4 * j - i, :, lanes] = v
 
 
 def inverse_y(planes, table, out, result, sem):
@@ -368,6 +370,7 @@
             out_specs=VMEM,
             scratch_shapes=[
                 pltpu.VMEM((depth * SUB, width), jnp.float32),
+                pltpu.VMEM((depth * SUB, width), jnp.float32),
                 pltpu.VMEM((depth, LANES), jnp.float32),
                 pltpu.VMEM((depth * SUB, width), jnp.float32),
             ],

time: 62.1 us -> 62 us (level)
  no operation moved by 1% of the time
where the time goes in v3:
time: 62 us; the launch traced here: 61.8 us
  blocking collectives  23.3 us (38%)
  starting transfers between devices  15.6 us (25%)
  waiting for transfers between devices  14.6 us (24%)
  Pallas kernels  8.22 us (13%)
    all_to_all x1, blocking collectives, per_device(): returned = lax.all_to_all(spatial, ALL, 0, 0, tiled=True)  23.3 us
    all_to_all x1, starting transfers between devices, per_device(): lax.all_to_all(planes.reshape(devices, SUB, flat), ALL, 0, 0, tiled=True)  11.5 us
    all_to_all x1, waiting for transfers between devices, per_device(): lax.all_to_all(planes.reshape(devices, SUB, flat), ALL, 0, 0, tiled=True)  10.3 us
    ppermute x3, waiting for transfers between devices, per_device(): lax.ppermute(own, 'growth', [((j + k) % slabs, j) for j in range(slabs)])  4.32 us
    ppermute x3, starting transfers between devices, per_device(): lax.ppermute(own, 'growth', [((j + k) % slabs, j) for j in range(slabs)])  4.13 us
    pallas_call x1, Pallas kernels, per_device(): pl.pallas_call(forward_y, out_shape=shape(width, flat), in_specs=[HBM, HB...  3.6 us
    pallas_call x1, Pallas kernels, per_device(): pl.pallas_call(middle, out_shape=shape(devices, SUB, flat), in_specs=[VME...  2.68 us
    pallas_call x1, Pallas kernels, per_device(): pl.pallas_call(inverse_y, out_shape=shape(flat, width), in_specs=[VMEM] *...  1.93 us
  transfers between devices with their start and end apart: 4, of which 3 were waited for; matrix products, arithmetic and copies ran while one was open for 0% of the time, Pallas kernels for 0%

profile of v3, /device:TPU:1, one launch (start us, length us, event | category | flops | bytes accessed | tf_op | source)
XLA Modules:
  0.0 61.8 jit_solution(8957449132658057391)
XLA Ops:
  0.0 3.6 %forward_y.1 = f32[1024,256]{1,0:T(8,128)} custom-call(f32[256,1024]{1,0:T(8,128)} %bitcast.6, bf16[2048,512]{1,0:T(8,128)(2,1)} %constant.2.clone.table_hbm.table), custom_call_target="tpu_custom_call" | custom-call | tf_op jit(solution)/shard_map/forward_y/pallas_call | solution.py:349
  3.6 0.0 copy-start.1
  3.6 0.0 copy-start
  3.6 11.5 %all-to-all-start = ((f32[128,8,256]{2,1,0:T(8,128)}), f32[128,8,256]{2,1,0:T(8,128)S(1)}, u32[]{:S(2)}, u32[]{:S(2)}) async-start(f32[128,8,256]{2,1,0:T(8,128)} %bitcast.5), calls=%async_computation | async-start | bytes 2097152 | tf_op jit(solution)/shard_map/all_to_all | solution.py:365
  15.1 0.0 copy-done.1
  15.1 0.1 broadcast_in_dim.2.own
  15.2 3.2 %collective-permute-start = (f32[8,128]{1,0:T(8,128)S(1)}, f32[8,128]{1,0:T(8,128)S(1)}, u32[]{:S(2)}, u32[]{:S(2)}) collective-permute-start(f32[8,128]{1,0:T(8,128)S(1)} %broadcast_in_dim.2.own), channel_id=1, source_target_pairs={{32,0},{64,32},{96,64},{0,96},{33,1},{65,33},{97,65},{1,97},{34,2}... | collective-permute-start | bytes 12296 | tf_op jit(solution)/shard_map/ppermute | solution.py:346
  18.5 0.1 collective-permute-start.1
  18.6 0.8 %collective-permute-start.2 = (f32[8,128]{1,0:T(8,128)S(1)}, f32[8,128]{1,0:T(8,128)S(1)}, u32[]{:S(2)}, u32[]{:S(2)}) collective-permute-start(f32[8,128]{1,0:T(8,128)S(1)} %broadcast_in_dim.2.own), channel_id=1, source_target_pairs={{96,0},{0,32},{32,64},{64,96},{97,1},{1,33},{33,65},{65,97},{98,2}... | collective-permute-start | bytes 12296 | tf_op jit(solution)/shard_map/ppermute | solution.py:346
  19.3 0.0 collective-permute-done.next1
  19.4 4.3 %collective-permute-done.1.next2 = f32[8,128]{1,0:T(8,128)S(1)} collective-permute-done((f32[8,128]{1,0:T(8,128)S(1)}, f32[8,128]{1,0:T(8,128)S(1)}, u32[]{:S(2)}, u32[]{:S(2)}) %collective-permute-start.1) | collective-permute-done | bytes 4128 | tf_op jit(solution)/shard_map/ppermute | solution.py:346
  23.6 0.1 collective-permute-done.2.next3
  23.7 10.3 %all-to-all-done.moved = f32[128,8,256]{2,1,0:T(8,128)S(1)} async-done(((f32[128,8,256]{2,1,0:T(8,128)}), f32[128,8,256]{2,1,0:T(8,128)S(1)}, u32[]{:S(2)}, u32[]{:S(2)}) %all-to-all-start) | async-done | bytes 1048608 | tf_op jit(solution)/shard_map/all_to_all | solution.py:365
  33.9 0.0 copy-done
  33.9 2.7 %middle.1 = f32[128,8,256]{2,1,0:T(8,128)S(1)} custom-call(f32[128,8,256]{2,1,0:T(8,128)S(1)} %all-to-all-done.moved, bf16[2048,512]{1,0:T(8,128)(2,1)S(1)} %copy-done, f32[8,128]{1,0:T(8,128)S(1)} %broadcast_in_dim.2.own, f32[8,128]{1,0:T(8,128)S(1)} %collective-permute-done.next1, f32[8,128]{1,0:T(8,128)S(1)} %collective-permute-done.1.next2, ...), custom_call_target="tpu_custom_call" | custom-call | tf_op jit(solution)/shard_map/middle/pallas_call | solution.py:366
  36.6 23.3 %all_to_all.10 = f32[128,8,256]{2,1,0:T(8,128)S(1)} all-to-all(f32[128,8,256]{2,1,0:T(8,128)S(1)} %middle.1), channel_id=1, replica_groups=mesh['growth'=4,'lat'=32] {'growth','lat'}, dimensions={0} | all-to-all | bytes 2097152 | tf_op jit(solution)/shard_map/all_to_all | solution.py:380
  59.9 1.9 %inverse_y.1 = f32[256,1024]{1,0:T(8,128)} custom-call(f32[1024,256]{1,0:T(8,128)S(1)} %bitcast.4, bf16[2048,512]{1,0:T(8,128)(2,1)S(1)} %copy-done), custom_call_target="tpu_custom_call" | custom-call | tf_op jit(solution)/shard_map/inverse_y/pallas_call | solution.py:381
Async XLA Ops:
  3.6 11.5 %copy-start.1 = (f32[8]{0:T(128)S(1)}, f32[8]{0:T(128)}, u32[]{:S(2)}) copy-start(f32[8]{0:T(128)} %param.4) | copy-start | bytes 100
  3.6 30.3 %copy-start = (bf16[2048,512]{1,0:T(8,128)(2,1)S(1)}, bf16[2048,512]{1,0:T(8,128)(2,1)}, u32[]{:S(2)}) copy-start(bf16[2048,512]{1,0:T(8,128)(2,1)} %constant.2.clone.table_hbm.table) | copy-start | bytes 6291460
  3.6 30.3 %all-to-all-start = ((f32[128,8,256]{2,1,0:T(8,128)}), f32[128,8,256]{2,1,0:T(8,128)S(1)}, u32[]{:S(2)}, u32[]{:S(2)}) async-start(f32[128,8,256]{2,1,0:T(8,128)} %bitcast.5), calls=%async_computation | async-start | bytes 2097152 | tf_op jit(solution)/shard_map/all_to_all | solution.py:365
  15.2 4.1 %collective-permute-start = (f32[8,128]{1,0:T(8,128)S(1)}, f32[8,128]{1,0:T(8,128)S(1)}, u32[]{:S(2)}, u32[]{:S(2)}) collective-permute-start(f32[8,128]{1,0:T(8,128)S(1)} %broadcast_in_dim.2.own), channel_id=1, source_target_pairs={{32,0},{64,32},{96,64},{0,96},{33,1},{65,33},{97,65},{1,97},{34,2}... | collective-permute-start | bytes 12296 | tf_op jit(solution)/shard_map/ppermute | solution.py:346
  18.5 5.2 %collective-permute-start.1 = (f32[8,128]{1,0:T(8,128)S(1)}, f32[8,128]{1,0:T(8,128)S(1)}, u32[]{:S(2)}, u32[]{:S(2)}) collective-permute-start(f32[8,128]{1,0:T(8,128)S(1)} %broadcast_in_dim.2.own), channel_id=1, source_target_pairs={{64,0},{96,32},{0,64},{32,96},{65,1},{97,33},{1,65},{33,97},{66,2}... | collective-permute-start | bytes 12296 | tf_op jit(solution)/shard_map/ppermute | solution.py:346
  18.6 5.1 %collective-permute-start.2 = (f32[8,128]{1,0:T(8,128)S(1)}, f32[8,128]{1,0:T(8,128)S(1)}, u32[]{:S(2)}, u32[]{:S(2)}) collective-permute-start(f32[8,128]{1,0:T(8,128)S(1)} %broadcast_in_dim.2.own), channel_id=1, source_target_pairs={{96,0},{0,32},{32,64},{64,96},{97,1},{1,33},{33,65},{65,97},{98,2}... | collective-permute-start | bytes 12296 | tf_op jit(solution)/shard_map/ppermute | solution.py:346

commit v4 on v3

--- a/solution.py
+++ b/solution.py
@@ -17,12 +17,14 @@
 
 
 def mode_order(points):
-    return np.concatenate([np.arange(0, points, 2), np.arange(1, points, 2)])
-
-
-def half_table(points):
-    k = mode_order(points)[:, None].astype(np.int64)
-    j = np.arange(points // 2, dtype=np.int64)[None, :]
+    return np.concatenate(
+        [np.arange(0, points, 4), np.arange(2, points, 4), np.arange(1, points, 2)]
+    )
+
+
+def part_table(points, modes, columns):
+    k = modes[:, None].astype(np.int64)
+    j = np.arange(columns, dtype=np.int64)[None, :]
     angle = ((2 * j + 1) * k % (4 * points)).astype(np.float64) * (math.pi / (2.0 * points))
     scale = np.where(k == 0, math.sqrt(1.0 / points), math.sqrt(2.0 / points))
     table = (scale * np.cos(angle)).astype(np.float32)
@@ -31,6 +33,12 @@
     return np.concatenate([high, low], axis=0)
 
 
+def tables(points):
+    modes = mode_order(points)
+    half = points // 2
+    return part_table(points, modes[:half], half // 2), part_table(points, modes[half:], half)
+
+
 def quarter_sine(angle):
     square = angle * angle
     value = 1.0 - square * (1.0 / 156.0)
@@ -41,7 +49,9 @@
 
 def eigenvalue(slot, points):
     half = points // 2
-    mode = jnp.where(slot < half, 2 * slot, 2 * (slot - half) + 1)
+    quarter = points // 4
+    even = jnp.where(slot < quarter, 4 * slot, 4 * (slot - quarter) + 2)
+    mode = jnp.where(slot < half, even, 2 * (slot - half) + 1)
     sine = quarter_sine(mode.astype(jnp.float32) * (math.pi / (2.0 * points)))
     return 4.0 * sine * sine
 
@@ -68,11 +78,12 @@
     return both[:count] + (one(left[0], right[1]) + both[count:])
 
 
-def parity(table, which):
-    n = table.shape[0] // 4
+def fold(tiles):
+    count = len(tiles) // 2
+    mirrored = [reverse_lanes(tiles[-1 - j], LANES) for j in range(count)]
     return (
-        table[which * n : (which + 1) * n, :],
-        table[(2 + which) * n : (3 + which) * n, :],
+        [tiles[j] + mirrored[j] for j in range(count)],
+        [tiles[j] - mirrored[j] for j in range(count)],
     )
 
 
@@ -82,42 +93,40 @@
     return jnp.take_along_axis(value, source, axis=1)
 
 
-def forward_y(source, table_hbm, out_hbm, rows, table, out, sem, table_sem, out_sem):
-    flat, points = rows.shape
+def forward_y(
+    source, narrow_hbm, full_hbm, out_hbm, rows, narrow, full, out, sem, table_sem, out_sem
+):
+    points = rows.shape[1]
     half = points // 2
-    tiles = half // LANES
-    pieces = 4
-    step = points // pieces
+    quarter = half // 2
     fetch = pltpu.make_async_copy(source, rows, sem)
     fetch.start()
 
-    def table_copy(i):
-        at = pl.ds(pl.multiple_of((i % 2) * points + (i // 2) * half, half), half)
-        return pltpu.make_async_copy(table_hbm.at[at, :], table.at[at, :], table_sem.at[i])
-
-    @pl.loop(0, 4)
+    def table_copy(i, from_ref, to_ref):
+        at = pl.ds(pl.multiple_of((i % 2) * half, half), half)
+        return pltpu.make_async_copy(from_ref.at[at, :], to_ref.at[at, :], table_sem.at[i])
+
+    @pl.loop(0, 2)
     def _(i):
-        table_copy(i).start()
+        table_copy(i, narrow_hbm, narrow).start()
+
+    @pl.loop(2, 4)
+    def _(i):
+        table_copy(i, full_hbm, full).start()
 
     fetch.wait()
-    first = [rows[:, pl.ds(j * LANES, LANES)] for j in range(tiles)]
-    second = [
-        reverse_lanes(rows[:, pl.ds((2 * tiles - 1 - j) * LANES, LANES)], LANES)
-        for j in range(tiles)
-    ]
-    folded = (
-        split(jnp.concatenate([a + b for a, b in zip(first, second)], axis=1)),
-        split(jnp.concatenate([a - b for a, b in zip(first, second)], axis=1)),
-    )
+    even, odd = fold([rows[:, pl.ds(j * LANES, LANES)] for j in range(points // LANES)])
+    parts = [split(jnp.concatenate(tiles, axis=1)) for tiles in (*fold(even), odd, odd)]
     copies = []
-    for i in range(pieces):
-        which = i * 2 // pieces
-        if i % (pieces // 2) == 0:
-            table_copy(2 * which).wait()
-            table_copy(2 * which + 1).wait()
-        at = pl.ds(i * step, step)
-        low = pl.ds(points + i * step, step)
-        out[at, :] = product((table[at, :], table[low, :]), folded[which], NT)
+    for i in range(4):
+        from_ref, to_ref = (narrow_hbm, narrow) if i < 2 else (full_hbm, full)
+        if i % 2 == 0:
+            table_copy(i, from_ref, to_ref).wait()
+            table_copy(i + 1, from_ref, to_ref).wait()
+        high = pl.ds((i % 2) * quarter, quarter)
+        low = pl.ds(half + (i % 2) * quarter, quarter)
+        at = pl.ds(i * quarter, quarter)
+        out[at, :] = product((to_ref[high, :], to_ref[low, :]), parts[i], NT)
         copies.append(pltpu.make_async_copy(out.at[at, :], out_hbm.at[at, :], out_sem.at[i]))
         copies[-1].start()
     for copy in copies:
@@ -184,7 +193,7 @@
 
 
 def middle(
-    moved, table, own, next1, next2, next3, out, rows, modal, heights, inverse
+    moved, narrow, full, own, next1, next2, next3, out, rows, modal, heights, inverse
 ):
     slabs = 4
     pivots(own, next1, next2, next3, heights, inverse)
@@ -193,14 +202,25 @@
     lat = moved.shape[0] // slabs
     width = rows.shape[1]
     half = width // 2
+    quarter = half // 2
     tiles = half // LANES
     lane = lax.broadcasted_iota(jnp.int32, (SUB, LANES), 1)
     chunks = 2
     span = half // chunks
     blocks = [(g, s) for g in range(slabs) for s in range(2)]
 
-    def part(which, high):
-        return pl.ds((0 if high else width) + which * half, half)
+    def place(g, s, q):
+        return pl.ds((g * slab + s * 4 + q) * SUB, SUB)
+
+    def narrow_part(which):
+        return (
+            narrow[pl.ds(which * quarter, quarter), :],
+            narrow[pl.ds(half + which * quarter, quarter), :],
+        )
+
+    def full_part(c):
+        at = pl.ds(c * span, span)
+        return full[pl.ds(0, half), at], full[pl.ds(half, half), at]
 
     for c in range(chunks):
         for g, s in blocks:
@@ -215,15 +235,22 @@
                     True,
                 )
                 for q in range(4):
-                    at = pl.ds((g * slab + s * 4 + q) * SUB, SUB)
+                    at = place(g, s, q)
                     rows[at, pl.ds(j * LANES, LANES)] = first[q] + second[q]
                     rows[at, pl.ds(half + j * LANES, LANES)] = first[q] - second[q]
-        at = pl.ds(c * span, span)
-        for which in range(2):
-            data = split(rows[:, pl.ds(which * half + c * span, span)])
-            value = shared(data, (table[part(which, 1), at], table[part(which, 0), at]), NT)
-            to = pl.ds(which * half, half)
-            modal[:, to] = value if c == 0 else modal[:, to] + value
+        data = split(rows[:, pl.ds(half + c * span, span)])
+        value = shared(data, full_part(c), NT)
+        to = pl.ds(half, half)
+        modal[:, to] = value if c == 0 else modal[:, to] + value
+    for g, s in blocks:
+        for q in range(4):
+            at = place(g, s, q)
+            even = fold([rows[at, pl.ds(j * LANES, LANES)] for j in range(tiles)])
+            for j, tile in enumerate(even[0] + even[1]):
+                rows[at, pl.ds(j * LANES, LANES)] = tile
+    for which in range(2):
+        at = pl.ds(which * quarter, quarter)
+        modal[:, at] = shared(split(rows[:, at]), narrow_part(which), NT)
 
     h = [heights[z : z + 1, :] for z in range(depth)]
     conduct = conductances(h)
@@ -244,29 +271,33 @@
             solved = modal[at, lanes] + wide(conduct[z + 1], half) * inverse[at, lanes] * solved
             modal[at, lanes] = solved
 
-    def inverse_x(which, data, c):
-        at = pl.ds(c * span, span)
-        rows[:, pl.ds(which * half + c * span, span)] = shared(
-            data, (table[part(which, 1), at], table[part(which, 0), at]), NN
-        )
-
-    solve(0)
-    even = split(modal[:, pl.ds(0, half)])
-    for c in range(chunks):
-        inverse_x(0, even, c)
     solve(1)
     odd = split(modal[:, pl.ds(half, half)])
     for c in range(chunks):
-        inverse_x(1, odd, c)
+        rows[:, pl.ds(half + c * span, span)] = shared(odd, full_part(c), NN)
+    solve(0)
+    for which in range(2):
+        at = pl.ds(which * quarter, quarter)
+        rows[:, at] = shared(split(modal[:, at]), narrow_part(which), NN)
+    for g, s in blocks:
+        for q in range(4):
+            at = place(g, s, q)
+            tile = [rows[at, pl.ds(j * LANES, LANES)] for j in range(tiles)]
+            count = tiles // 2
+            for j in range(count):
+                rows[at, pl.ds(j * LANES, LANES)] = tile[j] + tile[count + j]
+                rows[at, pl.ds((tiles - 1 - j) * LANES, LANES)] = reverse_lanes(
+                    tile[j] - tile[count + j], LANES
+                )
+    for c in range(chunks):
         for g, s in blocks:
             lanes = pl.ds(s * LANES, LANES)
             for j in range(c * tiles // chunks, (c + 1) * tiles // chunks):
                 first = []
                 second = []
                 for q in range(4):
-                    where = pl.ds((g * slab + s * 4 + q) * SUB, SUB)
-                    a = rows[where, pl.ds(j * LANES, LANES)]
-                    b = rows[where, pl.ds(half + j * LANES, LANES)]
+                    a = rows[place(g, s, q), pl.ds(j * LANES, LANES)]
+                    b = rows[place(g, s, q), pl.ds(half + j * LANES, LANES)]
                     first.append(a + b)
                     second.append(a - b)
                 for i, v in enumerate(swap_groups(first, lane, False)):
@@ -275,42 +306,51 @@
                     out[g * lat + lat - 1 - 4 * j - i, :, lanes] = v
 
 
-def inverse_y(planes, table, out, result, sem):
+def mirror(value):
+    count = value.shape[1] // LANES
+    return jnp.concatenate(
+        [
+            reverse_lanes(value[:, (count - 1 - j) * LANES : (count - j) * LANES], LANES)
+            for j in range(count)
+        ],
+        axis=1,
+    )
+
+
+def inverse_y(planes, narrow, full, out, result, sem):
     points = planes.shape[0]
     half = points // 2
-    chunks = 2
-    span = half // chunks
-    tiles = span // LANES
-    data = [split(planes[pl.ds(which * half, half), :].T) for which in range(2)]
+    quarter = half // 2
     copies = []
 
-    def send(at):
+    def send(start):
+        at = pl.ds(start, quarter)
         copies.append(
             pltpu.make_async_copy(result.at[:, at], out.at[:, at], sem.at[len(copies)])
         )
         copies[-1].start()
 
-    for c in range(chunks):
-        at = pl.ds(c * span, span)
-        even, odd = (
-            shared(
-                data[which],
-                (
-                    table[pl.ds(which * half, half), at],
-                    table[pl.ds(points + which * half, half), at],
-                ),
-                NN,
-            )
-            for which in range(2)
+    sums, differences = (
+        shared(
+            split(planes[pl.ds(which * quarter, quarter), :].T),
+            (
+                narrow[pl.ds(which * quarter, quarter), :],
+                narrow[pl.ds(half + which * quarter, quarter), :],
+            ),
+            NN,
         )
+        for which in range(2)
+    )
+    data = split(planes[pl.ds(half, half), :].T)
+    for c in range(2):
+        at = pl.ds(c * quarter, quarter)
+        odd = shared(data, (full[pl.ds(0, half), at], full[pl.ds(half, half), at]), NN)
+        even = sums + differences if c == 0 else mirror(sums - differences)
         result[:, at] = even + odd
-        send(at)
-        rest = even - odd
-        mirror = points - (c + 1) * span
-        for j in range(tiles):
-            lanes = slice((tiles - 1 - j) * LANES, (tiles - j) * LANES)
-            result[:, pl.ds(mirror + j * LANES, LANES)] = reverse_lanes(rest[:, lanes], LANES)
-        send(pl.ds(mirror, span))
+        send(c * quarter)
+        other = points - (c + 1) * quarter
+        result[:, pl.ds(other, quarter)] = mirror(even - odd)
+        send(other)
     for copy in copies:
         copy.wait()
 
@@ -340,7 +380,7 @@
         flat = slab * xlocal
         half = width // 2
         depth = slab * slabs
-        table = jnp.asarray(half_table(width))
+        narrow, full = (jnp.asarray(a) for a in tables(width))
         own = jnp.broadcast_to(spacing[:, None], (slab, LANES))
         others = [
             lax.ppermute(own, "growth", [((j + k) % slabs, j) for j in range(slabs)])
@@ -349,11 +389,12 @@
         planes = pl.pallas_call(
             forward_y,
             out_shape=shape(width, flat),
-            in_specs=[HBM, HBM],
+            in_specs=[HBM, HBM, HBM],
             out_specs=HBM,
             scratch_shapes=[
                 pltpu.VMEM((flat, width), jnp.float32),
-                pltpu.VMEM((2 * width, half), jnp.bfloat16),
+                pltpu.VMEM((width, half // 2), jnp.bfloat16),
+                pltpu.VMEM((width, half), jnp.bfloat16),
                 pltpu.VMEM((width, flat), jnp.float32),
                 pltpu.SemaphoreType.DMA,
                 pltpu.SemaphoreType.DMA((4,)),
@@ -361,12 +402,12 @@
             ],
             compiler_params=limit(FULL),
             name="forward_y",
-        )(source.reshape(flat, width), table)
+        )(source.reshape(flat, width), narrow, full)
         moved = lax.all_to_all(planes.reshape(devices, SUB, flat), ALL, 0, 0, tiled=True)
         spatial = pl.pallas_call(
             middle,
             out_shape=shape(devices, SUB, flat),
-            in_specs=[VMEM] * 6,
+            in_specs=[VMEM] * 7,
             out_specs=VMEM,
             scratch_shapes=[
                 pltpu.VMEM((depth * SUB, width), jnp.float32),
@@ -376,12 +417,12 @@
             ],
             compiler_params=limit(24 << 20),
             name="middle",
-        )(moved, table, own, *others)
+        )(moved, narrow, full, own, *others)
         returned = lax.all_to_all(spatial, ALL, 0, 0, tiled=True)
         result = pl.pallas_call(
             inverse_y,
             out_shape=shape(flat, width),
-            in_specs=[VMEM] * 2,
+            in_specs=[VMEM] * 3,
             out_specs=HBM,
             scratch_shapes=[
                 pltpu.VMEM((flat, width), jnp.float32),
@@ -389,7 +430,7 @@
             ],
             compiler_params=limit(24 << 20),
             name="inverse_y",
-        )(returned.reshape(width, flat), table)
+        )(returned.reshape(width, flat), narrow, full)
         return result.reshape(slab, xlocal, width)
 
     return jax.shard_map(

time: 62 us -> 61.8 us (level)
  no operation moved by 1% of the time
where the time goes in v4:
time: 61.8 us; the launch traced here: 61.6 us
  blocking collectives  23.3 us (38%)
  starting transfers between devices  15.6 us (25%)
  waiting for transfers between devices  14.6 us (24%)
  Pallas kernels  8.02 us (13%)
    all_to_all x1, blocking collectives, per_device(): returned = lax.all_to_all(spatial, ALL, 0, 0, tiled=True)  23.3 us
    all_to_all x1, starting transfers between devices, per_device(): lax.all_to_all(planes.reshape(devices, SUB, flat), ALL, 0, 0, tiled=True)  11.5 us
    all_to_all x1, waiting for transfers between devices, per_device(): lax.all_to_all(planes.reshape(devices, SUB, flat), ALL, 0, 0, tiled=True)  10.3 us
    ppermute x3, waiting for transfers between devices, per_device(): lax.ppermute(own, 'growth', [((j + k) % slabs, j) for j in range(slabs)])  4.32 us
    ppermute x3, starting transfers between devices, per_device(): lax.ppermute(own, 'growth', [((j + k) % slabs, j) for j in range(slabs)])  4.13 us
    pallas_call x1, Pallas kernels, per_device(): pl.pallas_call(forward_y, out_shape=shape(width, flat), in_specs=[HBM, HB...  3.44 us
    pallas_call x1, Pallas kernels, per_device(): pl.pallas_call(middle, out_shape=shape(devices, SUB, flat), in_specs=[VME...  2.67 us
    pallas_call x1, Pallas kernels, per_device(): pl.pallas_call(inverse_y, out_shape=shape(flat, width), in_specs=[VMEM] *...  1.91 us
  transfers between devices with their start and end apart: 4, of which 3 were waited for; matrix products, arithmetic and copies ran while one was open for 0% of the time, Pallas kernels for 0%

profile of v4, /device:TPU:1, one launch (start us, length us, event | category | flops | bytes accessed | tf_op | source)
XLA Modules:
  0.0 61.6 jit_solution(16853673239943866020)
XLA Ops:
  0.0 3.4 %forward_y.1 = f32[1024,256]{1,0:T(8,128)} custom-call(f32[256,1024]{1,0:T(8,128)} %bitcast.6, bf16[1024,256]{1,0:T(8,128)(2,1)} %constant.4.clone.narrow_hbm.narrow, bf16[1024,512]{1,0:T(8,128)(2,1)} %constant.5.clone.full_hbm.full), custom_call_target="tpu_custom_call" | custom-call | tf_op jit(solution)/shard_map/forward_y/pallas_call | solution.py:389
  3.4 0.0 copy-start.2
  3.5 0.0 copy-start
  3.5 0.0 copy-start.1
  3.5 11.5 %all-to-all-start = ((f32[128,8,256]{2,1,0:T(8,128)}), f32[128,8,256]{2,1,0:T(8,128)S(1)}, u32[]{:S(2)}, u32[]{:S(2)}) async-start(f32[128,8,256]{2,1,0:T(8,128)} %bitcast.5), calls=%async_computation | async-start | bytes 2097152 | tf_op jit(solution)/shard_map/all_to_all | solution.py:406
  15.0 0.0 copy-done.2
  15.0 0.1 broadcast_in_dim.2.own
  15.1 3.2 %collective-permute-start = (f32[8,128]{1,0:T(8,128)S(1)}, f32[8,128]{1,0:T(8,128)S(1)}, u32[]{:S(2)}, u32[]{:S(2)}) collective-permute-start(f32[8,128]{1,0:T(8,128)S(1)} %broadcast_in_dim.2.own), channel_id=1, source_target_pairs={{32,0},{64,32},{96,64},{0,96},{33,1},{65,33},{97,65},{1,97},{34,2}... | collective-permute-start | bytes 12296 | tf_op jit(solution)/shard_map/ppermute | solution.py:386
  18.3 0.1 collective-permute-start.1
  18.4 0.8 %collective-permute-start.2 = (f32[8,128]{1,0:T(8,128)S(1)}, f32[8,128]{1,0:T(8,128)S(1)}, u32[]{:S(2)}, u32[]{:S(2)}) collective-permute-start(f32[8,128]{1,0:T(8,128)S(1)} %broadcast_in_dim.2.own), channel_id=1, source_target_pairs={{96,0},{0,32},{32,64},{64,96},{97,1},{1,33},{33,65},{65,97},{98,2}... | collective-permute-start | bytes 12296 | tf_op jit(solution)/shard_map/ppermute | solution.py:386
  19.2 0.0 collective-permute-done.next1
  19.2 4.3 %collective-permute-done.1.next2 = f32[8,128]{1,0:T(8,128)S(1)} collective-permute-done((f32[8,128]{1,0:T(8,128)S(1)}, f32[8,128]{1,0:T(8,128)S(1)}, u32[]{:S(2)}, u32[]{:S(2)}) %collective-permute-start.1) | collective-permute-done | bytes 4128 | tf_op jit(solution)/shard_map/ppermute | solution.py:386
  23.5 0.1 collective-permute-done.2.next3
  23.5 10.3 %all-to-all-done.moved = f32[128,8,256]{2,1,0:T(8,128)S(1)} async-done(((f32[128,8,256]{2,1,0:T(8,128)}), f32[128,8,256]{2,1,0:T(8,128)S(1)}, u32[]{:S(2)}, u32[]{:S(2)}) %all-to-all-start) | async-done | bytes 1048608 | tf_op jit(solution)/shard_map/all_to_all | solution.py:406
  33.8 0.0 copy-done
  33.8 0.0 copy-done.1
  33.8 2.7 %middle.1 = f32[128,8,256]{2,1,0:T(8,128)S(1)} custom-call(f32[128,8,256]{2,1,0:T(8,128)S(1)} %all-to-all-done.moved, bf16[1024,256]{1,0:T(8,128)(2,1)S(1)} %copy-done.1, bf16[1024,512]{1,0:T(8,128)(2,1)S(1)} %copy-done, f32[8,128]{1,0:T(8,128)S(1)} %broadcast_in_dim.2.own, f32[8,128]{1,0:T(8,128)S(1)} %collective-permute-done.next1, ...), custom_call_target="tpu_custom_call" | custom-call | tf_op jit(solution)/shard_map/middle/pallas_call | solution.py:407
  36.4 23.3 %all_to_all.10 = f32[128,8,256]{2,1,0:T(8,128)S(1)} all-to-all(f32[128,8,256]{2,1,0:T(8,128)S(1)} %middle.1), channel_id=1, replica_groups=mesh['growth'=4,'lat'=32] {'growth','lat'}, dimensions={0} | all-to-all | bytes 2097152 | tf_op jit(solution)/shard_map/all_to_all | solution.py:421
  59.7 1.9 %inverse_y.1 = f32[256,1024]{1,0:T(8,128)} custom-call(f32[1024,256]{1,0:T(8,128)S(1)} %bitcast.4, bf16[1024,256]{1,0:T(8,128)(2,1)S(1)} %copy-done.1, bf16[1024,512]{1,0:T(8,128)(2,1)S(1)} %copy-done), custom_call_target="tpu_custom_call" | custom-call | tf_op jit(solution)/shard_map/inverse_y/pallas_call | solution.py:422
Async XLA Ops:
  3.4 11.5 %copy-start.2 = (f32[8]{0:T(128)S(1)}, f32[8]{0:T(128)}, u32[]{:S(2)}) copy-start(f32[8]{0:T(128)} %param.5) | copy-start | bytes 100
  3.5 30.3 %copy-start = (bf16[1024,512]{1,0:T(8,128)(2,1)S(1)}, bf16[1024,512]{1,0:T(8,128)(2,1)}, u32[]{:S(2)}) copy-start(bf16[1024,512]{1,0:T(8,128)(2,1)} %constant.5.clone.full_hbm.full) | copy-start | bytes 3145732
  3.5 30.3 %copy-start.1 = (bf16[1024,256]{1,0:T(8,128)(2,1)S(1)}, bf16[1024,256]{1,0:T(8,128)(2,1)}, u32[]{:S(2)}) copy-start(bf16[1024,256]{1,0:T(8,128)(2,1)} %constant.4.clone.narrow_hbm.narrow) | copy-start | bytes 1572868
  3.5 30.3 %all-to-all-start = ((f32[128,8,256]{2,1,0:T(8,128)}), f32[128,8,256]{2,1,0:T(8,128)S(1)}, u32[]{:S(2)}, u32[]{:S(2)}) async-start(f32[128,8,256]{2,1,0:T(8,128)} %bitcast.5), calls=%async_computation | async-start | bytes 2097152 | tf_op jit(solution)/shard_map/all_to_all | solution.py:406
  15.1 4.1 %collective-permute-start = (f32[8,128]{1,0:T(8,128)S(1)}, f32[8,128]{1,0:T(8,128)S(1)}, u32[]{:S(2)}, u32[]{:S(2)}) collective-permute-start(f32[8,128]{1,0:T(8,128)S(1)} %broadcast_in_dim.2.own), channel_id=1, source_target_pairs={{32,0},{64,32},{96,64},{0,96},{33,1},{65,33},{97,65},{1,97},{34,2}... | collective-permute-start | bytes 12296 | tf_op jit(solution)/shard_map/ppermute | solution.py:386
  18.3 5.2 %collective-permute-start.1 = (f32[8,128]{1,0:T(8,128)S(1)}, f32[8,128]{1,0:T(8,128)S(1)}, u32[]{:S(2)}, u32[]{:S(2)}) collective-permute-start(f32[8,128]{1,0:T(8,128)S(1)} %broadcast_in_dim.2.own), channel_id=1, source_target_pairs={{64,0},{96,32},{0,64},{32,96},{65,1},{97,33},{1,65},{33,97},{66,2}... | collective-permute-start | bytes 12296 | tf_op jit(solution)/shard_map/ppermute | solution.py:386
  18.4 5.1 %collective-permute-start.2 = (f32[8,128]{1,0:T(8,128)S(1)}, f32[8,128]{1,0:T(8,128)S(1)}, u32[]{:S(2)}, u32[]{:S(2)}) collective-permute-start(f32[8,128]{1,0:T(8,128)S(1)} %broadcast_in_dim.2.own), channel_id=1, source_target_pairs={{96,0},{0,32},{32,64},{64,96},{97,1},{1,33},{33,65},{65,97},{98,2}... | collective-permute-start | bytes 12296 | tf_op jit(solution)/shard_map/ppermute | solution.py:386

commit v5 on v4

--- a/solution.py
+++ b/solution.py
@@ -93,6 +93,12 @@
     return jnp.take_along_axis(value, source, axis=1)
 
 
+def turned_cells(slab):
+    own = lax.rem(lax.axis_index("lat"), 4)
+    cells = [4 * (p // 4) + lax.rem(p % 4 + 4 - own, 4) for p in range(slab)]
+    return [pl.multiple_of(cell * GROUP, GROUP) for cell in cells]
+
+
 def forward_y(
     source, narrow_hbm, full_hbm, out_hbm, rows, narrow, full, out, sem, table_sem, out_sem
 ):
@@ -115,7 +121,13 @@
         table_copy(i, full_hbm, full).start()
 
     fetch.wait()
-    even, odd = fold([rows[:, pl.ds(j * LANES, LANES)] for j in range(points // LANES)])
+    starts = turned_cells(rows.shape[0] // GROUP)
+
+    def column(j):
+        lanes = pl.ds(j * LANES, LANES)
+        return jnp.concatenate([rows[pl.ds(at, GROUP), lanes] for at in starts], axis=0)
+
+    even, odd = fold([column(j) for j in range(points // LANES)])
     parts = [split(jnp.concatenate(tiles, axis=1)) for tiles in (*fold(even), odd, odd)]
     copies = []
     for i in range(4):
@@ -133,28 +145,29 @@
         copy.wait()
 
 
-def permute(value, source):
-    return jnp.take_along_axis(value, source, axis=1)
-
-
-def exchange(a, b, keep, source, turn=None):
-    moved = jnp.where(keep, b, a)
-    moved = pltpu.roll(moved, LANES // 2, 1) if source is None else permute(moved, source)
-    if turn is None:
-        return jnp.where(keep, a, moved), jnp.where(keep, moved, b)
-    kept = permute(jnp.where(keep, a, b), turn)
-    return jnp.where(keep, kept, moved), jnp.where(keep, moved, kept)
-
-
-def swap_groups(v, lane, reverse):
-    keep = lane < 2 * GROUP
-    t0, t2 = exchange(v[0], v[2], keep, None)
-    t1, t3 = exchange(v[1], v[3], keep, None)
-    keep = lane // GROUP % 2 == 0
-    w = exchange(t0, t1, keep, lane ^ GROUP) + exchange(t2, t3, keep, lane ^ GROUP)
-    if reverse:
-        w = tuple(permute(x, lane ^ (GROUP - 1)) for x in w)
-    return w
+def pick(tiles, lane):
+    group = lane // GROUP
+    upper = jnp.where(group == 2, tiles[2], tiles[3])
+    return jnp.where(group < 2, jnp.where(group == 0, tiles[0], tiles[1]), upper)
+
+
+def turn(value, count):
+    return pltpu.roll(value, GROUP * (count % 4), 1) if count % 4 else value
+
+
+def collect(v, lane, reverse):
+    if not reverse:
+        return [turn(pick([v[(p - q) % 4] for p in range(4)], lane), -q) for q in range(4)]
+    picked = [pick([v[(q + 3 - p) % 4] for p in range(4)], lane) for q in range(4)]
+    return [turn(reverse_lanes(tile, LANES), q) for q, tile in enumerate(picked)]
+
+
+def spread(w, lane, reverse):
+    if not reverse:
+        turned = [turn(tile, q) for q, tile in enumerate(w)]
+        return [pick([turned[(p - i) % 4] for p in range(4)], lane) for i in range(4)]
+    turned = [reverse_lanes(turn(tile, -q), LANES) for q, tile in enumerate(w)]
+    return [pick([turned[(i + p + 1) % 4] for p in range(4)], lane) for i in range(4)]
 
 
 def wide(row, width):
@@ -226,10 +239,10 @@
         for g, s in blocks:
             lanes = pl.ds(s * LANES, LANES)
             for j in range(c * tiles // chunks, (c + 1) * tiles // chunks):
-                first = swap_groups(
+                first = collect(
                     [moved[g * lat + 4 * j + i, :, lanes] for i in range(4)], lane, False
                 )
-                second = swap_groups(
+                second = collect(
                     [moved[g * lat + lat - 1 - 4 * j - i, :, lanes] for i in range(4)],
                     lane,
                     True,
@@ -300,9 +313,9 @@
                     b = rows[place(g, s, q), pl.ds(half + j * LANES, LANES)]
                     first.append(a + b)
                     second.append(a - b)
-                for i, v in enumerate(swap_groups(first, lane, False)):
+                for i, v in enumerate(spread(first, lane, False)):
                     out[g * lat + 4 * j + i, :, lanes] = v
-                for i, v in enumerate(swap_groups(second, lane, True)):
+                for i, v in enumerate(spread(second, lane, True)):
                     out[g * lat + lat - 1 - 4 * j - i, :, lanes] = v
 
 
@@ -323,8 +336,12 @@
     quarter = half // 2
     copies = []
 
-    def send(start):
+    starts = turned_cells(result.shape[0] // GROUP)
+
+    def send(start, value):
         at = pl.ds(start, quarter)
+        for p, row in enumerate(starts):
+            result[pl.ds(row, GROUP), at] = value[p * GROUP : (p + 1) * GROUP, :]
         copies.append(
             pltpu.make_async_copy(result.at[:, at], out.at[:, at], sem.at[len(copies)])
         )
@@ -346,11 +363,8 @@
         at = pl.ds(c * quarter, quarter)
         odd = shared(data, (full[pl.ds(0, half), at], full[pl.ds(half, half), at]), NN)
         even = sums + differences if c == 0 else mirror(sums - differences)
-        result[:, at] = even + odd
-        send(c * quarter)
-        other = points - (c + 1) * quarter
-        result[:, pl.ds(other, quarter)] = mirror(even - odd)
-        send(other)
+        send(c * quarter, even + odd)
+        send(points - (c + 1) * quarter, mirror(even - odd))
     for copy in copies:
         copy.wait()
 

time: 61.8 us -> 61.3 us (level)
  no operation moved by 1% of the time
where the time goes in v5:
time: 61.3 us; the launch traced here: 61.2 us
  blocking collectives  23.3 us (38%)
  starting transfers between devices  15.6 us (25%)
  waiting for transfers between devices  14.6 us (24%)
  Pallas kernels  7.55 us (12%)
    all_to_all x1, blocking collectives, per_device(): returned = lax.all_to_all(spatial, ALL, 0, 0, tiled=True)  23.3 us
    all_to_all x1, starting transfers between devices, per_device(): lax.all_to_all(planes.reshape(devices, SUB, flat), ALL, 0, 0, tiled=True)  11.5 us
    all_to_all x1, waiting for transfers between devices, per_device(): lax.all_to_all(planes.reshape(devices, SUB, flat), ALL, 0, 0, tiled=True)  10.3 us
    ppermute x3, waiting for transfers between devices, per_device(): lax.ppermute(own, 'growth', [((j + k) % slabs, j) for j in range(slabs)])  4.32 us
    ppermute x3, starting transfers between devices, per_device(): lax.ppermute(own, 'growth', [((j + k) % slabs, j) for j in range(slabs)])  4.13 us
    pallas_call x1, Pallas kernels, per_device(): pl.pallas_call(forward_y, out_shape=shape(width, flat), in_specs=[HBM, HB...  3.44 us
    pallas_call x1, Pallas kernels, per_device(): pl.pallas_call(middle, out_shape=shape(devices, SUB, flat), in_specs=[VME...  2.21 us
    pallas_call x1, Pallas kernels, per_device(): pl.pallas_call(inverse_y, out_shape=shape(flat, width), in_specs=[VMEM] *...  1.9 us
  transfers between devices with their start and end apart: 4, of which 3 were waited for; matrix products, arithmetic and copies ran while one was open for 0% of the time, Pallas kernels for 0%

profile of v5, /device:TPU:1, one launch (start us, length us, event | category | flops | bytes accessed | tf_op | source)
XLA Modules:
  0.0 61.2 jit_solution(6775752349067292607)
XLA Ops:
  0.0 3.4 %forward_y.1 = f32[1024,256]{1,0:T(8,128)} custom-call(f32[256,1024]{1,0:T(8,128)} %bitcast.6, bf16[1024,256]{1,0:T(8,128)(2,1)} %constant.4.clone.narrow_hbm.narrow, bf16[1024,512]{1,0:T(8,128)(2,1)} %constant.5.clone.full_hbm.full), custom_call_target="tpu_custom_call" | custom-call | tf_op jit(solution)/shard_map/forward_y/pallas_call | solution.py:403
  3.4 0.0 copy-start.2
  3.5 0.0 copy-start
  3.5 0.0 copy-start.1
  3.5 11.5 %all-to-all-start = ((f32[128,8,256]{2,1,0:T(8,128)}), f32[128,8,256]{2,1,0:T(8,128)S(1)}, u32[]{:S(2)}, u32[]{:S(2)}) async-start(f32[128,8,256]{2,1,0:T(8,128)} %bitcast.5), calls=%async_computation | async-start | bytes 2097152 | tf_op jit(solution)/shard_map/all_to_all | solution.py:420
  15.0 0.0 copy-done.2
  15.0 0.1 broadcast_in_dim.2.own
  15.1 3.2 %collective-permute-start = (f32[8,128]{1,0:T(8,128)S(1)}, f32[8,128]{1,0:T(8,128)S(1)}, u32[]{:S(2)}, u32[]{:S(2)}) collective-permute-start(f32[8,128]{1,0:T(8,128)S(1)} %broadcast_in_dim.2.own), channel_id=1, source_target_pairs={{32,0},{64,32},{96,64},{0,96},{33,1},{65,33},{97,65},{1,97},{34,2}... | collective-permute-start | bytes 12296 | tf_op jit(solution)/shard_map/ppermute | solution.py:400
  18.3 0.1 collective-permute-start.1
  18.4 0.8 %collective-permute-start.2 = (f32[8,128]{1,0:T(8,128)S(1)}, f32[8,128]{1,0:T(8,128)S(1)}, u32[]{:S(2)}, u32[]{:S(2)}) collective-permute-start(f32[8,128]{1,0:T(8,128)S(1)} %broadcast_in_dim.2.own), channel_id=1, source_target_pairs={{96,0},{0,32},{32,64},{64,96},{97,1},{1,33},{33,65},{65,97},{98,2}... | collective-permute-start | bytes 12296 | tf_op jit(solution)/shard_map/ppermute | solution.py:400
  19.2 0.0 collective-permute-done.next1
  19.2 4.3 %collective-permute-done.1.next2 = f32[8,128]{1,0:T(8,128)S(1)} collective-permute-done((f32[8,128]{1,0:T(8,128)S(1)}, f32[8,128]{1,0:T(8,128)S(1)}, u32[]{:S(2)}, u32[]{:S(2)}) %collective-permute-start.1) | collective-permute-done | bytes 4128 | tf_op jit(solution)/shard_map/ppermute | solution.py:400
  23.5 0.1 collective-permute-done.2.next3
  23.5 10.3 %all-to-all-done.moved = f32[128,8,256]{2,1,0:T(8,128)S(1)} async-done(((f32[128,8,256]{2,1,0:T(8,128)}), f32[128,8,256]{2,1,0:T(8,128)S(1)}, u32[]{:S(2)}, u32[]{:S(2)}) %all-to-all-start) | async-done | bytes 1048608 | tf_op jit(solution)/shard_map/all_to_all | solution.py:420
  33.8 0.0 copy-done
  33.8 0.0 copy-done.1
  33.8 2.2 %middle.1 = f32[128,8,256]{2,1,0:T(8,128)S(1)} custom-call(f32[128,8,256]{2,1,0:T(8,128)S(1)} %all-to-all-done.moved, bf16[1024,256]{1,0:T(8,128)(2,1)S(1)} %copy-done.1, bf16[1024,512]{1,0:T(8,128)(2,1)S(1)} %copy-done, f32[8,128]{1,0:T(8,128)S(1)} %broadcast_in_dim.2.own, f32[8,128]{1,0:T(8,128)S(1)} %collective-permute-done.next1, ...), custom_call_target="tpu_custom_call" | custom-call | tf_op jit(solution)/shard_map/middle/pallas_call | solution.py:421
  36.0 23.3 %all_to_all.10 = f32[128,8,256]{2,1,0:T(8,128)S(1)} all-to-all(f32[128,8,256]{2,1,0:T(8,128)S(1)} %middle.1), channel_id=1, replica_groups=mesh['growth'=4,'lat'=32] {'growth','lat'}, dimensions={0} | all-to-all | bytes 2097152 | tf_op jit(solution)/shard_map/all_to_all | solution.py:435
  59.3 1.9 %inverse_y.1 = f32[256,1024]{1,0:T(8,128)} custom-call(f32[1024,256]{1,0:T(8,128)S(1)} %bitcast.4, bf16[1024,256]{1,0:T(8,128)(2,1)S(1)} %copy-done.1, bf16[1024,512]{1,0:T(8,128)(2,1)S(1)} %copy-done), custom_call_target="tpu_custom_call" | custom-call | tf_op jit(solution)/shard_map/inverse_y/pallas_call | solution.py:436
Async XLA Ops:
  3.4 11.5 %copy-start.2 = (f32[8]{0:T(128)S(1)}, f32[8]{0:T(128)}, u32[]{:S(2)}) copy-start(f32[8]{0:T(128)} %param.5) | copy-start | bytes 100
  3.5 30.3 %copy-start = (bf16[1024,512]{1,0:T(8,128)(2,1)S(1)}, bf16[1024,512]{1,0:T(8,128)(2,1)}, u32[]{:S(2)}) copy-start(bf16[1024,512]{1,0:T(8,128)(2,1)} %constant.5.clone.full_hbm.full) | copy-start | bytes 3145732
  3.5 30.3 %copy-start.1 = (bf16[1024,256]{1,0:T(8,128)(2,1)S(1)}, bf16[1024,256]{1,0:T(8,128)(2,1)}, u32[]{:S(2)}) copy-start(bf16[1024,256]{1,0:T(8,128)(2,1)} %constant.4.clone.narrow_hbm.narrow) | copy-start | bytes 1572868
  3.5 30.3 %all-to-all-start = ((f32[128,8,256]{2,1,0:T(8,128)}), f32[128,8,256]{2,1,0:T(8,128)S(1)}, u32[]{:S(2)}, u32[]{:S(2)}) async-start(f32[128,8,256]{2,1,0:T(8,128)} %bitcast.5), calls=%async_computation | async-start | bytes 2097152 | tf_op jit(solution)/shard_map/all_to_all | solution.py:420
  15.1 4.1 %collective-permute-start = (f32[8,128]{1,0:T(8,128)S(1)}, f32[8,128]{1,0:T(8,128)S(1)}, u32[]{:S(2)}, u32[]{:S(2)}) collective-permute-start(f32[8,128]{1,0:T(8,128)S(1)} %broadcast_in_dim.2.own), channel_id=1, source_target_pairs={{32,0},{64,32},{96,64},{0,96},{33,1},{65,33},{97,65},{1,97},{34,2}... | collective-permute-start | bytes 12296 | tf_op jit(solution)/shard_map/ppermute | solution.py:400
  18.3 5.2 %collective-permute-start.1 = (f32[8,128]{1,0:T(8,128)S(1)}, f32[8,128]{1,0:T(8,128)S(1)}, u32[]{:S(2)}, u32[]{:S(2)}) collective-permute-start(f32[8,128]{1,0:T(8,128)S(1)} %broadcast_in_dim.2.own), channel_id=1, source_target_pairs={{64,0},{96,32},{0,64},{32,96},{65,1},{97,33},{1,65},{33,97},{66,2}... | collective-permute-start | bytes 12296 | tf_op jit(solution)/shard_map/ppermute | solution.py:400
  18.4 5.1 %collective-permute-start.2 = (f32[8,128]{1,0:T(8,128)S(1)}, f32[8,128]{1,0:T(8,128)S(1)}, u32[]{:S(2)}, u32[]{:S(2)}) collective-permute-start(f32[8,128]{1,0:T(8,128)S(1)} %broadcast_in_dim.2.own), channel_id=1, source_target_pairs={{96,0},{0,32},{32,64},{64,96},{97,1},{1,33},{33,65},{65,97},{98,2}... | collective-permute-start | bytes 12296 | tf_op jit(solution)/shard_map/ppermute | solution.py:400
